TPU v7x, 32 devices: a whole 2x2x4 slice. The times are simulated.
32 devices in a mesh: scen: 2 (over y), dw: 4 (over x, core), reg: 4 (over z).
Axes of the slice: x: 2, y: 2, z: 4, core: 2. Of those that a mesh axis runs over, the one named last changes fastest.
Arguments:
- load_base: float32 [96, 65536], P(None, ('scen', 'dw', 'reg')), parts along dimension 1, may hold values from -24 to 24
- kkt_inverse: float32 [64, 96, 96], replicated, may hold values from -1 to 2
- archetype: int32 [65536], P(('scen', 'dw', 'reg')), parts along dimension 0, may hold values from 0 to 63
- feeder: int32 [65536], P(('scen', 'dw', 'reg')), parts along dimension 0, may hold values from 0 to 255, as said below
- live_counts: int32 [32, 4], P(('scen', 'dw', 'reg')), parts along dimension 0, may hold values from 1 to 512, as said below
- feeder_cap: int32 [512], P(('scen', 'dw', 'reg')), parts along dimension 0, may hold values from 1000 to 11999
- dual_start: float32 [512, 96], P(('scen', 'dw', 'reg')), parts along dimension 0, may hold values from 0 to 1
- balance_target: float32 [192], P('scen'), parts along dimension 0, may hold values from -6 to 6
Outputs:
- roster: float32 [96, 65536], P(None, ('scen', 'dw', 'reg')), parts along dimension 1
- feeder_duals: float32 [512, 96], P(('scen', 'dw', 'reg')), parts along dimension 0
- balance_dual: float32 [192], P('scen'), parts along dimension 0
There are 2 independent parts, one for each index of `scen`. A program takes and returns all parts, laid end to end along the dimension named above; an argument that names none is the same for every part. Nothing has to cross between parts.
Inputs may be any that keep to these rules, and one draw needn't show every extreme that they name: The feeder of the dwelling in slot s of the device at index j along dw and r along reg lies in block k * 4 + r of 16 feeders, where k = s // 512. `live_counts`: row d (devices in the order dw+reg) gives for each block k the number of leading slots of that block that hold a dwelling; the other slots are empty. Every row has a block of 512.
All inputs are finite; a program needn't handle non-finite values.
Results may differ from a plain program's by a relative error of at most 0.0003.
Values sent between devices are 32-bit elements; how exact they have to be, the bound alone decides.
No kernel may reach another device: no remote copies, remote signals or barrier semaphores. Data moves between devices by JAX's collectives and lax.ppermute only.
A program may use at most 64 MiB of HBM per device.

v0:
```python
import math

import jax
import jax.numpy as jnp
from jax import lax
from jax.sharding import PartitionSpec as P

ITERS = 2


rho_weight = 0.5
dual_rate = 0.1
balance_rate = 1.0


def apply_inverse(kkt_inverse, archetype, rhs_field, block_width):
    steps_count, rows_count = rhs_field.shape
    block_count = rows_count // block_width
    blocks_in = rhs_field.reshape(steps_count, block_count, block_width).transpose(1, 0, 2)
    labels_in = archetype.reshape(block_count, block_width)

    def one_block(operand):
        labels, columns_in = operand
        picked = jnp.take(kkt_inverse, labels, axis=0)
        return jnp.einsum("bts,sb->tb", picked, columns_in, precision=lax.Precision.HIGHEST)

    out_blocks = lax.map(one_block, (labels_in, blocks_in))
    return out_blocks.transpose(1, 0, 2).reshape(steps_count, rows_count)


def on_device(
    load_base, kkt_inverse, archetype, feeder, live_counts, feeder_cap, dual_start, balance_target
):
    steps_count, rows_count = load_base.shape
    block_total = lax.axis_size("dw")
    slot_width = rows_count // block_total
    owned_count = dual_start.shape[0]
    slot_index = jnp.arange(slot_width, dtype=jnp.int32)
    live_mask = (
        (live_counts.reshape(block_total, 1) > slot_index[None, :])
        .reshape(rows_count)
        .astype(jnp.float32)
    )
    all_rows = rows_count * block_total * lax.axis_size("reg")
    inv_root = 1.0 / math.sqrt(all_rows)
    block_width = math.gcd(rows_count, 256)
    local_label = feeder % owned_count
    cap_value = feeder_cap.astype(jnp.float32) * 0.001
    feeder_duals = dual_start
    balance_dual = jnp.zeros((steps_count,), jnp.float32)
    roster = jnp.zeros_like(load_base)
    contract_rows = (((0,), (1,)), ((), ()))
    arrived_labels = lax.all_to_all(local_label, "dw", split_axis=0, concat_axis=0, tiled=True)
    owner_table = (
        arrived_labels[:, None] == jnp.arange(owned_count, dtype=jnp.int32)[None, :]
    ).astype(jnp.float32)
    for sweep_index in range(ITERS):
        owner_rows = lax.dot_general(
            feeder_duals, owner_table, contract_rows, precision=lax.Precision.HIGHEST
        )
        dwelling_duals = lax.all_to_all(owner_rows, "dw", split_axis=1, concat_axis=1, tiled=True)
        rhs_field = load_base - dwelling_duals - balance_dual[:, None] + rho_weight * roster
        roster = apply_inverse(kkt_inverse, archetype, rhs_field, block_width) * live_mask[None, :]
        arrived_loads = lax.all_to_all(roster, "dw", split_axis=1, concat_axis=1, tiled=True)
        feeder_loads = lax.dot_general(
            owner_table, arrived_loads, contract_rows, precision=lax.Precision.HIGHEST
        )
        system_load = lax.psum(jnp.sum(feeder_loads, axis=0), ("dw", "reg"))
        feeder_duals = jnp.maximum(
            feeder_duals + dual_rate * (feeder_loads - cap_value[:, None]), 0.0
        )
        balance_dual = balance_dual + balance_rate * (system_load * inv_root - balance_target)
    return (roster, feeder_duals, balance_dual)


def solution(mesh):
    in_specs = (
        P(None, ("scen", "dw", "reg")),
        P(),
        P(("scen", "dw", "reg")),
        P(("scen", "dw", "reg")),
        P(("scen", "dw", "reg"), None),
        P(("scen", "dw", "reg")),
        P(("scen", "dw", "reg"), None),
        P("scen"),
    )
    out_specs = (P(None, ("scen", "dw", "reg")), P(("scen", "dw", "reg"), None), P("scen"))
    return jax.shard_map(
        on_device, mesh=mesh, in_specs=in_specs, out_specs=out_specs, check_vma=False
    )
```

profile of v0, /device:TPU:0, one launch (start us, length us, event | category | flops | bytes accessed | tf_op | source)
XLA Modules:
  0.0 417.4 jit_solution(971037340868108701)
XLA Ops:
  1.3 7.8 %all_to_all.51 = s32[4,512,1]{1,2,0:T(1,128)S(1)} all-to-all(s32[4,512,1]{1,2,0:T(1,128)S(1)} %bitcast.121), channel_id=1, replica_groups=mesh['scen'=2,'dw'=4,'reg'=4] {'dw'}, dimensions={0} | all-to-all | bytes 16384 | tf_op jit(solution)/shard_map/all_to_all | solution.py:53
  9.1 1.8 fusion.2
  11.9 3.5 all-to-all-start.1
  16.9 10.2 %all-to-all-done.1 = f32[96,4,512]{2,0,1:T(8,128)S(1)} async-done(((f32[96,4,512]{2,0,1:T(8,128)}), f32[96,4,512]{2,0,1:T(8,128)S(1)}, u32[]{:S(2)}, u32[]{:S(2)}) %all-to-all-start.1) | async-done | bytes 786464 | tf_op jit(solution)/shard_map/all_to_all | solution.py:61
  29.6 136.5 %while.20 = (s32[]{:T(128)}, f32[8,96,256]{2,1,0:T(8,128)}, f32[8,96,256]{2,0,1:T(8,128)S(1)}, s32[8,256]{1,0:T(8,128)S(1)}, f32[64,96,96]{2,1,0:T(8,128)}, /*index=5*/s32[]{:T(128)}) while((s32[]{:T(128)}, f32[8,96,256]{2,1,0:T(8,128)}, f32[8,96,256]{2,0,1:T(8,128)S(1)}, s32[8,256]{1,0:T(8,128)S(1)}, f32[64,96,96]{2,1,0:T(8,128)}, ...), condition=%wide.region_1.3_spmd, body=%wide.region_0.2_spmd.sunk | while | flops 7056642 | bytes 29306956 | solution.py:27
  29.6 7.8 %gather_fusion = f32[256,96,96]{2,1,0:T(8,128)} fusion(f32[64,96,96]{2,1,0:T(8,128)} %get-tuple-element.179, s32[1024]{0:T(1024)S(1)} %pad_clamp_fusion.4), kind=kCustom, calls=%fused_computation.clone.clone.1 | custom fusion | bytes 18875392 | tf_op jit(solution)/shard_map/while/body/eval_jaxpr/jit(_take)/gather | solution.py:24
  37.6 8.3 %multiply_reduce_fusion.4 = f32[256,96]{1,0:T(8,128)S(1)} fusion(f32[256,96,96]{2,1,0:T(8,128)} %gather_fusion, f32[256,96]{1,0:T(8,128)S(1)} %bitcast.87, pred[256]{0:T(512)(128)(4,1)S(1)} %compare_and_fusion.4), kind=kLoop, calls=%fused_computation.2.clone.1 | loop fusion | flops 7053312 | bytes 9634048 | tf_op jit(solution)/shard_map/while
  46.7 7.8 %gather_fusion = f32[256,96,96]{2,1,0:T(8,128)} fusion(f32[64,96,96]{2,1,0:T(8,128)} %get-tuple-element.179, s32[1024]{0:T(1024)S(1)} %pad_clamp_fusion.4), kind=kCustom, calls=%fused_computation.clone.clone.1 | custom fusion | bytes 18875392 | tf_op jit(solution)/shard_map/while/body/eval_jaxpr/jit(_take)/gather | solution.py:24
  54.7 8.3 %multiply_reduce_fusion.4 = f32[256,96]{1,0:T(8,128)S(1)} fusion(f32[256,96,96]{2,1,0:T(8,128)} %gather_fusion, f32[256,96]{1,0:T(8,128)S(1)} %bitcast.87, pred[256]{0:T(512)(128)(4,1)S(1)} %compare_and_fusion.4), kind=kLoop, calls=%fused_computation.2.clone.1 | loop fusion | flops 7053312 | bytes 9634048 | tf_op jit(solution)/shard_map/while
  63.7 7.8 %gather_fusion = f32[256,96,96]{2,1,0:T(8,128)} fusion(f32[64,96,96]{2,1,0:T(8,128)} %get-tuple-element.179, s32[1024]{0:T(1024)S(1)} %pad_clamp_fusion.4), kind=kCustom, calls=%fused_computation.clone.clone.1 | custom fusion | bytes 18875392 | tf_op jit(solution)/shard_map/while/body/eval_jaxpr/jit(_take)/gather | solution.py:24
  71.7 8.3 %multiply_reduce_fusion.4 = f32[256,96]{1,0:T(8,128)S(1)} fusion(f32[256,96,96]{2,1,0:T(8,128)} %gather_fusion, f32[256,96]{1,0:T(8,128)S(1)} %bitcast.87, pred[256]{0:T(512)(128)(4,1)S(1)} %compare_and_fusion.4), kind=kLoop, calls=%fused_computation.2.clone.1 | loop fusion | flops 7053312 | bytes 9634048 | tf_op jit(solution)/shard_map/while
  80.8 7.8 %gather_fusion = f32[256,96,96]{2,1,0:T(8,128)} fusion(f32[64,96,96]{2,1,0:T(8,128)} %get-tuple-element.179, s32[1024]{0:T(1024)S(1)} %pad_clamp_fusion.4), kind=kCustom, calls=%fused_computation.clone.clone.1 | custom fusion | bytes 18875392 | tf_op jit(solution)/shard_map/while/body/eval_jaxpr/jit(_take)/gather | solution.py:24
  88.8 8.3 %multiply_reduce_fusion.4 = f32[256,96]{1,0:T(8,128)S(1)} fusion(f32[256,96,96]{2,1,0:T(8,128)} %gather_fusion, f32[256,96]{1,0:T(8,128)S(1)} %bitcast.87, pred[256]{0:T(512)(128)(4,1)S(1)} %compare_and_fusion.4), kind=kLoop, calls=%fused_computation.2.clone.1 | loop fusion | flops 7053312 | bytes 9634048 | tf_op jit(solution)/shard_map/while
  97.8 7.8 %gather_fusion = f32[256,96,96]{2,1,0:T(8,128)} fusion(f32[64,96,96]{2,1,0:T(8,128)} %get-tuple-element.179, s32[1024]{0:T(1024)S(1)} %pad_clamp_fusion.4), kind=kCustom, calls=%fused_computation.clone.clone.1 | custom fusion | bytes 18875392 | tf_op jit(solution)/shard_map/while/body/eval_jaxpr/jit(_take)/gather | solution.py:24
  105.8 8.3 %multiply_reduce_fusion.4 = f32[256,96]{1,0:T(8,128)S(1)} fusion(f32[256,96,96]{2,1,0:T(8,128)} %gather_fusion, f32[256,96]{1,0:T(8,128)S(1)} %bitcast.87, pred[256]{0:T(512)(128)(4,1)S(1)} %compare_and_fusion.4), kind=kLoop, calls=%fused_computation.2.clone.1 | loop fusion | flops 7053312 | bytes 9634048 | tf_op jit(solution)/shard_map/while
  114.9 7.8 %gather_fusion = f32[256,96,96]{2,1,0:T(8,128)} fusion(f32[64,96,96]{2,1,0:T(8,128)} %get-tuple-element.179, s32[1024]{0:T(1024)S(1)} %pad_clamp_fusion.4), kind=kCustom, calls=%fused_computation.clone.clone.1 | custom fusion | bytes 18875392 | tf_op jit(solution)/shard_map/while/body/eval_jaxpr/jit(_take)/gather | solution.py:24
  122.9 8.3 %multiply_reduce_fusion.4 = f32[256,96]{1,0:T(8,128)S(1)} fusion(f32[256,96,96]{2,1,0:T(8,128)} %gather_fusion, f32[256,96]{1,0:T(8,128)S(1)} %bitcast.87, pred[256]{0:T(512)(128)(4,1)S(1)} %compare_and_fusion.4), kind=kLoop, calls=%fused_computation.2.clone.1 | loop fusion | flops 7053312 | bytes 9634048 | tf_op jit(solution)/shard_map/while
  131.9 7.8 %gather_fusion = f32[256,96,96]{2,1,0:T(8,128)} fusion(f32[64,96,96]{2,1,0:T(8,128)} %get-tuple-element.179, s32[1024]{0:T(1024)S(1)} %pad_clamp_fusion.4), kind=kCustom, calls=%fused_computation.clone.clone.1 | custom fusion | bytes 18875392 | tf_op jit(solution)/shard_map/while/body/eval_jaxpr/jit(_take)/gather | solution.py:24
  140.0 8.3 %multiply_reduce_fusion.4 = f32[256,96]{1,0:T(8,128)S(1)} fusion(f32[256,96,96]{2,1,0:T(8,128)} %gather_fusion, f32[256,96]{1,0:T(8,128)S(1)} %bitcast.87, pred[256]{0:T(512)(128)(4,1)S(1)} %compare_and_fusion.4), kind=kLoop, calls=%fused_computation.2.clone.1 | loop fusion | flops 7053312 | bytes 9634048 | tf_op jit(solution)/shard_map/while
  149.0 7.8 %gather_fusion = f32[256,96,96]{2,1,0:T(8,128)} fusion(f32[64,96,96]{2,1,0:T(8,128)} %get-tuple-element.179, s32[1024]{0:T(1024)S(1)} %pad_clamp_fusion.4), kind=kCustom, calls=%fused_computation.clone.clone.1 | custom fusion | bytes 18875392 | tf_op jit(solution)/shard_map/while/body/eval_jaxpr/jit(_take)/gather | solution.py:24
  157.0 8.3 %multiply_reduce_fusion.4 = f32[256,96]{1,0:T(8,128)S(1)} fusion(f32[256,96,96]{2,1,0:T(8,128)} %gather_fusion, f32[256,96]{1,0:T(8,128)S(1)} %bitcast.87, pred[256]{0:T(512)(128)(4,1)S(1)} %compare_and_fusion.4), kind=kLoop, calls=%fused_computation.2.clone.1 | loop fusion | flops 7053312 | bytes 9634048 | tf_op jit(solution)/shard_map/while
  166.0 2.6 copy.35
  168.7 2.4 reshape.77
  173.4 4.2 %all-to-all-start.2 = ((f32[96,4,512]{2,0,1:T(8,128)}), f32[96,4,512]{2,0,1:T(8,128)}, u32[]{:S(2)}, u32[]{:S(2)}) async-start(f32[96,4,512]{2,0,1:T(8,128)} %copy.36), calls=%async_computation.2 | async-start | bytes 1572864 | tf_op jit(solution)/shard_map/all_to_all | solution.py:64
  177.6 11.7 %all-to-all-done.2 = f32[96,4,512]{2,0,1:T(8,128)} async-done(((f32[96,4,512]{2,0,1:T(8,128)}), f32[96,4,512]{2,0,1:T(8,128)}, u32[]{:S(2)}, u32[]{:S(2)}) %all-to-all-start.2) | async-done | bytes 786464 | tf_op jit(solution)/shard_map/all_to_all | solution.py:64
  193.5 4.2 %all-to-all-start.3 = ((f32[96,4,512]{2,0,1:T(8,128)}), f32[96,4,512]{2,0,1:T(8,128)}, u32[]{:S(2)}, u32[]{:S(2)}) async-start(f32[96,4,512]{2,0,1:T(8,128)} %bitcast.91), calls=%async_computation.3 | async-start | bytes 1572864 | tf_op jit(solution)/shard_map/all_to_all | solution.py:61
  197.7 2.1 copy.68
  199.9 34.7 %psum.14 = f32[96]{0:T(128)S(1)} all-reduce(f32[96]{0:T(128)S(1)} %get-tuple-element.99), channel_id=1, replica_groups=mesh['scen'=2,'dw'=4,'reg'=4] {'dw','reg'}, use_global_device_ids=true, to_apply=%region_3.5 | all-reduce | flops 96 | bytes 768 | tf_op jit(solution)/shard_map/psum | solution.py:68
  239.3 127.9 %while.21 = (s32[]{:T(128)}, f32[8,96,256]{2,1,0:T(8,128)}, f32[8,96,256]{2,1,0:T(8,128)}, s32[8,256]{1,0:T(8,128)S(1)}, f32[64,96,96]{2,1,0:T(8,128)S(1)}, /*index=5*/s32[]{:T(128)}) while((s32[]{:T(128)}, f32[8,96,256]{2,1,0:T(8,128)}, f32[8,96,256]{2,1,0:T(8,128)}, s32[8,256]{1,0:T(8,128)S(1)}, f32[64,96,96]{2,1,0:T(8,128)S(1)}, ...), condition=%wide.region_5.7_spmd, body=%wide.region_4.6_spmd.sunk | while | flops 7056642 | bytes 29306956 | solution.py:27
  239.3 5.9 %gather_fusion.1 = f32[256,96,96]{2,1,0:T(8,128)} fusion(f32[64,96,96]{2,1,0:T(8,128)S(1)} %get-tuple-element.197, s32[1024]{0:T(1024)S(1)} %pad_clamp_fusion.5), kind=kCustom, calls=%fused_computation.1.clone.clone.1 | custom fusion | bytes 18875392 | tf_op jit(solution)/shard_map/while/body/eval_jaxpr/jit(_take)/gather | solution.py:24
  246.3 8.3 %multiply_reduce_fusion.5 = f32[256,96]{1,0:T(8,128)S(1)} fusion(f32[256,96,96]{2,1,0:T(8,128)} %gather_fusion.1, f32[256,96]{1,0:T(8,128)S(1)} %copy.85, pred[256]{0:T(512)(128)(4,1)S(1)} %compare_and_fusion.5), kind=kLoop, calls=%fused_computation.9.clone.1 | loop fusion | flops 7053312 | bytes 9634048 | tf_op jit(solution)/shard_map/while
  255.3 5.9 %gather_fusion.1 = f32[256,96,96]{2,1,0:T(8,128)} fusion(f32[64,96,96]{2,1,0:T(8,128)S(1)} %get-tuple-element.197, s32[1024]{0:T(1024)S(1)} %pad_clamp_fusion.5), kind=kCustom, calls=%fused_computation.1.clone.clone.1 | custom fusion | bytes 18875392 | tf_op jit(solution)/shard_map/while/body/eval_jaxpr/jit(_take)/gather | solution.py:24
  262.3 8.3 %multiply_reduce_fusion.5 = f32[256,96]{1,0:T(8,128)S(1)} fusion(f32[256,96,96]{2,1,0:T(8,128)} %gather_fusion.1, f32[256,96]{1,0:T(8,128)S(1)} %copy.85, pred[256]{0:T(512)(128)(4,1)S(1)} %compare_and_fusion.5), kind=kLoop, calls=%fused_computation.9.clone.1 | loop fusion | flops 7053312 | bytes 9634048 | tf_op jit(solution)/shard_map/while
  271.3 5.9 %gather_fusion.1 = f32[256,96,96]{2,1,0:T(8,128)} fusion(f32[64,96,96]{2,1,0:T(8,128)S(1)} %get-tuple-element.197, s32[1024]{0:T(1024)S(1)} %pad_clamp_fusion.5), kind=kCustom, calls=%fused_computation.1.clone.clone.1 | custom fusion | bytes 18875392 | tf_op jit(solution)/shard_map/while/body/eval_jaxpr/jit(_take)/gather | solution.py:24
  278.3 8.3 %multiply_reduce_fusion.5 = f32[256,96]{1,0:T(8,128)S(1)} fusion(f32[256,96,96]{2,1,0:T(8,128)} %gather_fusion.1, f32[256,96]{1,0:T(8,128)S(1)} %copy.85, pred[256]{0:T(512)(128)(4,1)S(1)} %compare_and_fusion.5), kind=kLoop, calls=%fused_computation.9.clone.1 | loop fusion | flops 7053312 | bytes 9634048 | tf_op jit(solution)/shard_map/while
  287.3 5.9 %gather_fusion.1 = f32[256,96,96]{2,1,0:T(8,128)} fusion(f32[64,96,96]{2,1,0:T(8,128)S(1)} %get-tuple-element.197, s32[1024]{0:T(1024)S(1)} %pad_clamp_fusion.5), kind=kCustom, calls=%fused_computation.1.clone.clone.1 | custom fusion | bytes 18875392 | tf_op jit(solution)/shard_map/while/body/eval_jaxpr/jit(_take)/gather | solution.py:24
  294.2 8.3 %multiply_reduce_fusion.5 = f32[256,96]{1,0:T(8,128)S(1)} fusion(f32[256,96,96]{2,1,0:T(8,128)} %gather_fusion.1, f32[256,96]{1,0:T(8,128)S(1)} %copy.85, pred[256]{0:T(512)(128)(4,1)S(1)} %compare_and_fusion.5), kind=kLoop, calls=%fused_computation.9.clone.1 | loop fusion | flops 7053312 | bytes 9634048 | tf_op jit(solution)/shard_map/while
  303.3 5.9 %gather_fusion.1 = f32[256,96,96]{2,1,0:T(8,128)} fusion(f32[64,96,96]{2,1,0:T(8,128)S(1)} %get-tuple-element.197, s32[1024]{0:T(1024)S(1)} %pad_clamp_fusion.5), kind=kCustom, calls=%fused_computation.1.clone.clone.1 | custom fusion | bytes 18875392 | tf_op jit(solution)/shard_map/while/body/eval_jaxpr/jit(_take)/gather | solution.py:24
  310.2 8.3 %multiply_reduce_fusion.5 = f32[256,96]{1,0:T(8,128)S(1)} fusion(f32[256,96,96]{2,1,0:T(8,128)} %gather_fusion.1, f32[256,96]{1,0:T(8,128)S(1)} %copy.85, pred[256]{0:T(512)(128)(4,1)S(1)} %compare_and_fusion.5), kind=kLoop, calls=%fused_computation.9.clone.1 | loop fusion | flops 7053312 | bytes 9634048 | tf_op jit(solution)/shard_map/while
  319.3 5.9 %gather_fusion.1 = f32[256,96,96]{2,1,0:T(8,128)} fusion(f32[64,96,96]{2,1,0:T(8,128)S(1)} %get-tuple-element.197, s32[1024]{0:T(1024)S(1)} %pad_clamp_fusion.5), kind=kCustom, calls=%fused_computation.1.clone.clone.1 | custom fusion | bytes 18875392 | tf_op jit(solution)/shard_map/while/body/eval_jaxpr/jit(_take)/gather | solution.py:24
  326.2 8.3 %multiply_reduce_fusion.5 = f32[256,96]{1,0:T(8,128)S(1)} fusion(f32[256,96,96]{2,1,0:T(8,128)} %gather_fusion.1, f32[256,96]{1,0:T(8,128)S(1)} %copy.85, pred[256]{0:T(512)(128)(4,1)S(1)} %compare_and_fusion.5), kind=kLoop, calls=%fused_computation.9.clone.1 | loop fusion | flops 7053312 | bytes 9634048 | tf_op jit(solution)/shard_map/while
  335.3 5.9 %gather_fusion.1 = f32[256,96,96]{2,1,0:T(8,128)} fusion(f32[64,96,96]{2,1,0:T(8,128)S(1)} %get-tuple-element.197, s32[1024]{0:T(1024)S(1)} %pad_clamp_fusion.5), kind=kCustom, calls=%fused_computation.1.clone.clone.1 | custom fusion | bytes 18875392 | tf_op jit(solution)/shard_map/while/body/eval_jaxpr/jit(_take)/gather | solution.py:24
  342.2 8.3 %multiply_reduce_fusion.5 = f32[256,96]{1,0:T(8,128)S(1)} fusion(f32[256,96,96]{2,1,0:T(8,128)} %gather_fusion.1, f32[256,96]{1,0:T(8,128)S(1)} %copy.85, pred[256]{0:T(512)(128)(4,1)S(1)} %compare_and_fusion.5), kind=kLoop, calls=%fused_computation.9.clone.1 | loop fusion | flops 7053312 | bytes 9634048 | tf_op jit(solution)/shard_map/while
  351.2 5.9 %gather_fusion.1 = f32[256,96,96]{2,1,0:T(8,128)} fusion(f32[64,96,96]{2,1,0:T(8,128)S(1)} %get-tuple-element.197, s32[1024]{0:T(1024)S(1)} %pad_clamp_fusion.5), kind=kCustom, calls=%fused_computation.1.clone.clone.1 | custom fusion | bytes 18875392 | tf_op jit(solution)/shard_map/while/body/eval_jaxpr/jit(_take)/gather | solution.py:24
  358.2 8.3 %multiply_reduce_fusion.5 = f32[256,96]{1,0:T(8,128)S(1)} fusion(f32[256,96,96]{2,1,0:T(8,128)} %gather_fusion.1, f32[256,96]{1,0:T(8,128)S(1)} %copy.85, pred[256]{0:T(512)(128)(4,1)S(1)} %compare_and_fusion.5), kind=kLoop, calls=%fused_computation.9.clone.1 | loop fusion | flops 7053312 | bytes 9634048 | tf_op jit(solution)/shard_map/while
  370.4 3.5 all-to-all-start.4
  376.1 9.5 %all-to-all-done.4 = f32[96,4,512]{2,0,1:T(8,128)S(1)} async-done(((f32[96,4,512]{2,0,1:T(8,128)}), f32[96,4,512]{2,0,1:T(8,128)S(1)}, u32[]{:S(2)}, u32[]{:S(2)}) %all-to-all-start.4) | async-done | bytes 786464 | tf_op jit(solution)/shard_map/all_to_all | solution.py:64
  387.3 29.7 %psum.15 = f32[96]{0:T(128)S(1)} all-reduce(f32[96]{0:T(128)S(1)} %get-tuple-element.95), channel_id=1, replica_groups=mesh['scen'=2,'dw'=4,'reg'=4] {'dw','reg'}, use_global_device_ids=true, to_apply=%region_7.9 | all-reduce | flops 96 | bytes 768 | tf_op jit(solution)/shard_map/psum | solution.py:68
  (169 shorter events, 46.0 us)
Async XLA Ops:
  11.9 15.1 %all-to-all-start.1 = ((f32[96,4,512]{2,0,1:T(8,128)}), f32[96,4,512]{2,0,1:T(8,128)S(1)}, u32[]{:S(2)}, u32[]{:S(2)}) async-start(f32[96,4,512]{2,0,1:T(8,128)} %bitcast.64), calls=%async_computation.1 | async-start | bytes 1572864 | tf_op jit(solution)/shard_map/all_to_all | solution.py:61
  29.6 148.1 %copy-start.3 = (s32[16]{0:T(128)S(1)}, s32[16]{0:T(128)}, u32[]{:S(2)}) copy-start(s32[16]{0:T(128)} %param.19) | copy-start | bytes 196
  29.6 162.0 %copy-start.1 = (f32[16,96]{1,0:T(8,128)S(1)}, f32[16,96]{1,0:T(8,128)}, u32[]{:S(2)}) copy-start(f32[16,96]{1,0:T(8,128)} %param.20) | copy-start | bytes 18436
  166.0 68.5 %copy-start.2 = (f32[96]{0:T(128)S(1)}, f32[96]{0:T(128)}, u32[]{:S(2)}) copy-start(f32[96]{0:T(128)} %param.21) | copy-start | bytes 1156
  166.0 73.3 %copy-start = (f32[64,96,96]{2,1,0:T(8,128)S(1)}, f32[64,96,96]{2,1,0:T(8,128)}, u32[]{:S(2)}) copy-start(f32[64,96,96]{2,1,0:T(8,128)} %get-tuple-element.199) | copy-start | bytes 7077892
  173.4 15.9 %all-to-all-start.2 = ((f32[96,4,512]{2,0,1:T(8,128)}), f32[96,4,512]{2,0,1:T(8,128)}, u32[]{:S(2)}, u32[]{:S(2)}) async-start(f32[96,4,512]{2,0,1:T(8,128)} %copy.36), calls=%async_computation.2 | async-start | bytes 1572864 | tf_op jit(solution)/shard_map/all_to_all | solution.py:64
  193.5 41.0 %all-to-all-start.3 = ((f32[96,4,512]{2,0,1:T(8,128)}), f32[96,4,512]{2,0,1:T(8,128)}, u32[]{:S(2)}, u32[]{:S(2)}) async-start(f32[96,4,512]{2,0,1:T(8,128)} %bitcast.91), calls=%async_computation.3 | async-start | bytes 1572864 | tf_op jit(solution)/shard_map/all_to_all | solution.py:61
  370.4 15.1 %all-to-all-start.4 = ((f32[96,4,512]{2,0,1:T(8,128)}), f32[96,4,512]{2,0,1:T(8,128)S(1)}, u32[]{:S(2)}, u32[]{:S(2)}) async-start(f32[96,4,512]{2,0,1:T(8,128)} %copy.44), calls=%async_computation.4 | async-start | bytes 1572864 | tf_op jit(solution)/shard_map/all_to_all | solution.py:64
where the time goes:
time: 419 us; the launch traced here: 417 us
  local copies, waits for them, and re-layouts  152 us (36%)
  other arithmetic  140 us (33%)
  blocking collectives  72.1 us (17%)
  waiting for transfers between devices  31.3 us (7%)
  starting transfers between devices  15.4 us (4%)
  matrix products  5.55 us (1%)
    while x16, other arithmetic  132 us
    gather x16, local copies, waits for them, and re-layouts, one_block(): picked = jnp.take(kkt_inverse, labels, axis=0)  110 us
    psum x2, blocking collectives, on_device(): system_load = lax.psum(jnp.sum(feeder_loads, axis=0), ('dw', 'reg'))  64.3 us
    all_to_all x2, waiting for transfers between devices, on_device(): lax.all_to_all(roster, 'dw', split_axis=1, concat_axis=1, tiled=True)  21.1 us
    dynamic_update_slice x16, local copies, waits for them, and re-layouts, apply_inverse(): out_blocks = lax.map(one_block, (labels_in, blocks_in))  10.5 us
    all_to_all x2, waiting for transfers between devices, on_device(): lax.all_to_all(owner_rows, 'dw', split_axis=1, concat_axis=1, tiled=True)  10.2 us
    while x24, local copies, waits for them, and re-layouts  8.65 us
  transfers between devices with their start and end apart: 4, of which 3 were waited for; matrix products, arithmetic and copies ran while one was open for 1% of the time, Pallas kernels for 0%

commit v1 on v0

v1 whole, which is shorter than its diff:
```python
import math

import jax
import jax.numpy as jnp
from jax import lax
from jax.experimental import pallas as pl
from jax.experimental.pallas import tpu as pltpu
from jax.sharding import PartitionSpec as P

rho_weight = 0.5
dual_rate = 0.1
balance_rate = 1.0

LANES = 128
ROWS = 256
WIN = 64
EXTRA = 32
VMEM_BYTES = 56 * 1024 * 1024

F32 = jnp.float32
BF16 = jnp.bfloat16
NT = (((1,), (1,)), ((), ()))
TN = (((0,), (0,)), ((), ()))


def iota(shape, dim):
    return lax.broadcasted_iota(jnp.int32, shape, dim)


def halves(x):
    high = x.astype(BF16)
    return high, (x - high.astype(F32)).astype(BF16)


def side(x):
    return jnp.concatenate(halves(x), axis=1)


def mm(a, b, dims=None):
    if dims is None:
        return jnp.dot(a, b, preferred_element_type=F32)
    return lax.dot_general(a, b, dims, preferred_element_type=F32)


def fold(x):
    return x[:, :LANES] + x[:, LANES:]


def feeder_hot(rows, steps, count):
    label = jnp.broadcast_to(rows[:, steps : steps + 1], (rows.shape[0], count))
    lane = iota((rows.shape[0], count), 1).astype(F32)
    return jnp.where(label == lane + 1.0, 1.0, 0.0).astype(BF16)


def split_matrices(kkt_ref, mat_ref):
    arch_count, steps, _ = kkt_ref.shape
    mat_ref[...] = jnp.zeros_like(mat_ref)
    for a in range(arch_count):
        high, low = halves(kkt_ref[a])
        mat_ref[a, 0:steps, 0:steps] = high
        mat_ref[a, LANES : LANES + steps, 0:steps] = low


def apply_matrix(x, matrix):
    count = x.shape[0]
    both = mm(jnp.concatenate(halves(x), axis=0), matrix, NT)
    return both[:count, :LANES] + (both[count:, :LANES] + both[:count, LANES:])


def each_group(offs_ref, arch_count, biggest, step):
    @pl.when(biggest <= WIN)
    def _():
        for a in range(arch_count):
            step(a, pl.multiple_of(offs_ref[0, a], 8))

    @pl.when(biggest > WIN)
    def _():
        def group(a, carry):
            start = offs_ref[0, a]

            def part(t, inner):
                step(a, pl.multiple_of(start + t * WIN, 8))
                return inner

            return lax.fori_loop(0, (offs_ref[1, a] + WIN - 1) // WIN, part, carry)

        lax.fori_loop(0, arch_count, group, 0)


def first_kernel(
    counts_ref, arch_ref, feeder_ref, load_ref, kkt_ref, duals_ref,
    y_ref, pos_ref, offs_ref, sums_ref,
    xt_ref, xs_ref, z_ref, r_ref, mat_ref, offs_smem,
):
    steps, rows_count = load_ref.shape
    arch_count = kkt_ref.shape[0]
    block_total = counts_ref.shape[1]
    feeders = duals_ref.shape[0]
    owned = feeders // block_total
    seg = rows_count // block_total
    lane = iota((1, rows_count), 1)
    bound = jnp.zeros((1, rows_count), jnp.int32)
    base = jnp.zeros((1, rows_count), jnp.int32)
    for k in range(block_total):
        inside = lane >= k * seg
        bound = jnp.where(inside, k * seg + counts_ref[0, k], bound)
        base = jnp.where(inside, k * owned, base)
    live = lane < bound
    kind = jnp.where(live, arch_ref[...], -1)
    label = jnp.where(live, lax.rem(feeder_ref[...], owned) + base + 1, 0).astype(F32)

    chunk = 256
    before = jnp.where(iota((chunk, chunk), 0) < iota((chunk, chunk), 1), 1.0, 0.0).astype(BF16)
    arch_iota = iota((arch_count, chunk), 0)
    carry = jnp.zeros((arch_count, 1), F32)
    hots, ranks = [], []
    for c in range(rows_count // chunk):
        hot = jnp.where(kind[:, c * chunk : (c + 1) * chunk] == arch_iota, 1.0, 0.0)
        ranks.append(mm(hot.astype(BF16), before) + carry)
        hots.append(hot)
        carry = carry + jnp.sum(hot, axis=1, keepdims=True)
    eights = jnp.floor((carry + 7.0) * 0.125)
    lower = jnp.where(iota((arch_count, arch_count), 1) < iota((arch_count, arch_count), 0), 1.0, 0.0).astype(BF16)
    offs = mm(lower, jnp.broadcast_to(eights, (arch_count, LANES)).astype(BF16)) * 8.0
    for c in range(rows_count // chunk):
        part = slice(c * chunk, (c + 1) * chunk)
        place = jnp.sum(hots[c] * (ranks[c] + offs[:, :1]), axis=0, keepdims=True)
        pos_ref[:, part] = jnp.where(live[:, part], place, -1.0).astype(jnp.int32)
    diagonal = iota((arch_count, LANES), 0) == iota((arch_count, LANES), 1)
    offs_row = jnp.sum(jnp.where(diagonal, offs, 0.0), axis=0, keepdims=True).astype(jnp.int32)
    size_row = jnp.sum(jnp.where(diagonal, jnp.broadcast_to(carry, (arch_count, LANES)), 0.0), axis=0, keepdims=True).astype(jnp.int32)
    offs_ref[...] = jnp.zeros_like(offs_ref)
    offs_ref[0:1, :] = offs_row
    offs_ref[1:2, :] = size_row
    biggest = jnp.max(carry).astype(jnp.int32)
    offs_ref[2:3, :] = jnp.full((1, LANES), biggest, jnp.int32)
    pltpu.sync_copy(offs_ref, offs_smem)

    split_matrices(kkt_ref, mat_ref)

    for c in range(rows_count // LANES):
        part = slice(c * LANES, (c + 1) * LANES)
        extra = jnp.where(iota((LANES - steps, LANES), 0) == 0, label[:, part], 0.0)
        block = jnp.concatenate([load_ref[:, part], extra], axis=0).T
        xt_ref[part, :] = side(block)

    duals_side = side(duals_ref[...])

    def permute(b, inner):
        at = pl.multiple_of(b * ROWS, ROWS)
        total = jnp.zeros((ROWS, 2 * LANES), F32)
        for c in range(rows_count // 512):
            part = slice(c * 512, (c + 1) * 512)
            hot = jnp.where(pos_ref[:, part] == iota((ROWS, 512), 0) + at, 1.0, 0.0).astype(BF16)
            total = total + mm(hot, xt_ref[part, :])
        xs = fold(total)
        xs_ref[pl.ds(at, ROWS), :] = xs
        z_ref[pl.ds(at, ROWS), :] = xs - fold(mm(feeder_hot(xs, steps, feeders), duals_side))
        r_ref[pl.ds(at, ROWS), :] = jnp.zeros((ROWS, LANES), F32)
        y_ref[pl.ds(at, ROWS), :] = jnp.zeros((ROWS, LANES), F32)
        return inner

    lax.fori_loop(0, xs_ref.shape[0] // ROWS, permute, 0)

    is_label = iota((WIN, LANES), 1) == steps

    def group(a, row):
        here = pl.ds(row, WIN)
        xs = xs_ref[here, :]
        matrix = mat_ref[a]
        r = apply_matrix(z_ref[here, :], matrix)
        r_ref[here, :] = r
        y = apply_matrix(xs + rho_weight * r, matrix)
        y_ref[here, :] = jnp.where(is_label, xs, y)

    each_group(offs_smem, arch_count, offs_smem[2, 0], group)

    def gather(b, total):
        at = pl.multiple_of(b * ROWS, ROWS)
        here = pl.ds(at, ROWS)
        row = iota((ROWS, LANES), 0) + at
        member = jnp.where((row >= offs_row) & (row < offs_row + size_row), 1.0, 0.0).astype(BF16)
        y = y_ref[here, :]
        right = jnp.concatenate([*halves(r_ref[here, :]), *halves(y), member], axis=1)
        return total + mm(feeder_hot(y, steps, feeders), right, TN)

    sums = lax.fori_loop(0, xs_ref.shape[0] // ROWS, gather, jnp.zeros((feeders, 5 * LANES), F32))
    sums_ref[:, 0:LANES] = sums[:, 0:LANES] + sums[:, LANES : 2 * LANES]
    sums_ref[:, LANES : 2 * LANES] = sums[:, 2 * LANES : 3 * LANES] + sums[:, 3 * LANES : 4 * LANES]
    sums_ref[:, 2 * LANES :] = sums[:, 4 * LANES :]


def middle_kernel(steps, arch_count, sums_ref, duals_ref, pack_ref, next_ref, rest_ref):
    total = sums_ref[0]
    for d in range(1, sums_ref.shape[0]):
        total = total + sums_ref[d]
    loads = total[:, :LANES]
    duals = duals_ref[...]
    cap = duals[:, steps : steps + 1]
    lane = iota(duals.shape, 1)
    after = jnp.maximum(duals + dual_rate * (loads - cap), 0.0)
    after = jnp.where(lane < steps, after, jnp.where(lane == steps, 1.0, 0.0))
    next_ref[...] = after
    rest_ref[...] = total[:, LANES:]
    mixed = lax.dot_general(
        total[:, 2 * LANES :], after, TN, precision=lax.Precision.HIGHEST, preferred_element_type=F32
    )
    pack_ref[0:arch_count, :] = mixed[:arch_count]
    row = iota((8, LANES), 0)
    load_sum = jnp.sum(loads, axis=0, keepdims=True)
    rest_sum = jnp.sum(total[:, LANES : 2 * LANES], axis=0, keepdims=True)
    pack_ref[arch_count:, :] = jnp.where(row == 0, load_sum, jnp.where(row == 1, rest_sum, 0.0))


def last_kernel(
    inv_root, owned, own_ref, offs_ref, y_ref, pos_ref, duals_ref, first_ref, rest_ref, left_ref, right_ref, kkt_ref, target_ref,
    out_ref, feeder_ref, balance_ref,
    z_ref, r_ref, side_ref, mat_ref, target_pad,
):
    arch_count, steps, _ = kkt_ref.shape
    rows_count = pos_ref.shape[1]
    feeders = duals_ref.shape[0]
    split_matrices(kkt_ref, mat_ref)
    pack = left_ref[...] + right_ref[...]
    target_pad[...] = jnp.zeros_like(target_pad)
    target_pad[0:1, 0:steps] = target_ref[...]
    target = target_pad[0:1, :]
    balance = balance_rate * (pack[arch_count : arch_count + 1] * inv_root - target)
    mixed = pack[:arch_count]
    mixed = mixed + mixed[:, steps : steps + 1] * balance
    duals_all = duals_ref[...] + balance
    duals_side = side(duals_all)
    own = pl.ds(pl.multiple_of(own_ref[0] * owned, owned), owned)
    own_before = duals_ref[own, :]
    own_duals = own_before + balance
    own_rest = rest_ref[own, :]

    def pick(b, inner):
        here = pl.ds(pl.multiple_of(b * ROWS, ROWS), ROWS)
        z_ref[here, :] = fold(mm(feeder_hot(y_ref[here, :], steps, feeders), duals_side))
        r_ref[here, :] = jnp.zeros((ROWS, LANES), F32)
        return inner

    lax.fori_loop(0, y_ref.shape[0] // ROWS, pick, 0)

    def group(a, row):
        here = pl.ds(row, WIN)
        r_ref[here, :] = y_ref[here, :] - apply_matrix(z_ref[here, :], mat_ref[a])

    each_group(offs_ref, arch_count, offs_ref[2, 0], group)

    acc = jnp.zeros((EXTRA, LANES), F32)
    first = iota((EXTRA - owned, LANES), 0) == 0
    for a in range(arch_count):
        rows = own_rest[:, LANES + a : LANES + a + 1] * own_duals
        more = jnp.where(first, mixed[a : a + 1], 0.0)
        acc = acc + apply_matrix(jnp.concatenate([rows, more], axis=0), mat_ref[a])

    loads = own_rest[:, :LANES] - acc[:owned]
    cap = first_ref[own, :][:, steps : steps + 1]
    after = jnp.maximum(own_before + dual_rate * (loads - cap), 0.0)
    feeder_ref[...] = after[:, :steps]
    system = pack[arch_count + 1 : arch_count + 2] - acc[owned : owned + 1]
    balance_ref[...] = (balance + balance_rate * (system * inv_root - target))[:, :steps]

    def split_rows(b, inner):
        here = pl.ds(pl.multiple_of(b * ROWS, ROWS), ROWS)
        side_ref[here, :] = side(r_ref[here, :])
        return inner

    lax.fori_loop(0, y_ref.shape[0] // ROWS, split_rows, 0)

    spread_rows = y_ref.shape[0]
    for c in range(rows_count // LANES):
        part = slice(c * LANES, (c + 1) * LANES)
        place = jnp.broadcast_to(pos_ref[:, part].astype(F32), (LANES, LANES)).T.astype(jnp.int32)
        total = jnp.zeros((LANES, 2 * LANES), F32)
        for k in range(spread_rows // 512):
            hot = jnp.concatenate(
                [
                    jnp.where(place == iota((LANES, LANES), 1) + (k * 512 + q * LANES), 1.0, 0.0).astype(BF16)
                    for q in range(4)
                ],
                axis=1,
            )
            total = total + mm(hot, side_ref[k * 512 : (k + 1) * 512, :])
        out_ref[:, part] = fold(total).T[:steps]


def vmem():
    return pl.BlockSpec(memory_space=pltpu.VMEM)


def smem():
    return pl.BlockSpec(memory_space=pltpu.SMEM)


def params():
    return pltpu.CompilerParams(vmem_limit_bytes=VMEM_BYTES)


def on_device(
    load_base, kkt_inverse, archetype, feeder, live_counts, feeder_cap, dual_start, balance_target
):
    steps, rows_count = load_base.shape
    arch_count = kkt_inverse.shape[0]
    block_total = lax.axis_size("dw")
    region_total = lax.axis_size("reg")
    owned = dual_start.shape[0]
    feeders = owned * block_total
    inv_root = 1.0 / math.sqrt(rows_count * block_total * region_total)
    space = -(-(rows_count + 7 * arch_count + WIN) // 512) * 512
    shape = jax.ShapeDtypeStruct

    cap = feeder_cap.astype(F32) * 0.001
    mine = jnp.concatenate(
        [dual_start, cap[:, None], jnp.zeros((owned, LANES - steps - 1), F32)], axis=1
    )
    duals = lax.all_gather(mine, "dw", axis=0, tiled=True)

    y, pos, offs, sums = pl.pallas_call(
        first_kernel,
        name="first",
        in_specs=[smem(), vmem(), vmem(), vmem(), vmem(), vmem()],
        out_specs=[vmem()] * 4,
        out_shape=[
            shape((space, LANES), F32),
            shape((1, rows_count), jnp.int32),
            shape((8, LANES), jnp.int32),
            shape((feeders, 3 * LANES), F32),
        ],
        scratch_shapes=[
            pltpu.VMEM((rows_count, 2 * LANES), BF16),
            pltpu.VMEM((space, LANES), F32),
            pltpu.VMEM((space, LANES), F32),
            pltpu.VMEM((space, LANES), F32),
            pltpu.VMEM((arch_count, 2 * LANES, LANES), BF16),
            pltpu.SMEM((8, LANES), jnp.int32),
        ],
        compiler_params=params(),
    )(
        live_counts,
        archetype.reshape(1, rows_count),
        feeder.reshape(1, rows_count),
        load_base,
        kkt_inverse,
        duals,
    )
    gathered = lax.all_gather(sums, "dw", axis=0)
    pack, next_duals, rest = pl.pallas_call(
        lambda *refs: middle_kernel(steps, arch_count, *refs),
        name="middle",
        in_specs=[vmem()] * 2,
        out_specs=[vmem()] * 3,
        out_shape=[
            shape((arch_count + 8, LANES), F32),
            shape((feeders, LANES), F32),
            shape((feeders, 2 * LANES), F32),
        ],
        compiler_params=params(),
    )(gathered, duals)
    stride = 1
    other = jnp.zeros_like(pack)
    while stride < region_total:
        if stride > 1:
            pack = pack + other
        other = lax.ppermute(pack, "reg", [(i, i ^ stride) for i in range(region_total)])
        stride *= 2
    own = lax.axis_index("dw").astype(jnp.int32).reshape(1)
    out, feeder_duals, balance_dual = pl.pallas_call(
        lambda *refs: last_kernel(inv_root, owned, *refs),
        name="last",
        in_specs=[smem(), smem()] + [vmem()] * 9,
        out_specs=[vmem()] * 3,
        out_shape=[
            shape((steps, rows_count), F32),
            shape((owned, steps), F32),
            shape((1, steps), F32),
        ],
        scratch_shapes=[
            pltpu.VMEM((space, LANES), F32),
            pltpu.VMEM((space, LANES), F32),
            pltpu.VMEM((space, 2 * LANES), BF16),
            pltpu.VMEM((arch_count, 2 * LANES, LANES), BF16),
            pltpu.VMEM((8, LANES), F32),
        ],
        compiler_params=params(),
    )(
        own, offs, y, pos, next_duals, duals, rest, pack, other, kkt_inverse,
        balance_target.reshape(1, steps),
    )
    return (out, feeder_duals, balance_dual.reshape(steps))


def solution(mesh):
    in_specs = (
        P(None, ("scen", "dw", "reg")),
        P(),
        P(("scen", "dw", "reg")),
        P(("scen", "dw", "reg")),
        P(("scen", "dw", "reg"), None),
        P(("scen", "dw", "reg")),
        P(("scen", "dw", "reg"), None),
        P("scen"),
    )
    out_specs = (P(None, ("scen", "dw", "reg")), P(("scen", "dw", "reg"), None), P("scen"))
    return jax.shard_map(
        on_device, mesh=mesh, in_specs=in_specs, out_specs=out_specs, check_vma=False
    )
```

time: 419 us -> 60.9 us (0.15)
  local copies, waits for them, and re-layouts: 152 us -> 0.77 us
  other arithmetic: 140 us -> 2.21 us
  blocking collectives: 72.1 us -> 15.5 us
  Pallas kernels: 0 us -> 32.4 us
  waiting for transfers between devices: 31.3 us -> 4.88 us
  starting transfers between devices: 15.4 us -> 4.14 us
  matrix products: 5.55 us -> 0 us
    while x16 -> x0, other arithmetic: 132 us -> none
    gather x16 -> x0, local copies, waits for them, and re-layouts: 110 us -> none  [one_block(): picked = jnp.take(kkt_inverse, labels, axis=0)]
    psum x2 -> x0, blocking collectives: 64.3 us -> none  [on_device(): system_load = lax.psum(jnp.sum(feeder_loads, axis=0), ('dw', 'reg'))]
    pallas_call x0 -> x3, Pallas kernels: none -> 32.4 us  [the longest x1 17.6 us: on_device(): pl.pallas_call(first_kernel, name='first', in_specs=[smem(), vmem(), vmem...]
    all_to_all x4 -> x0, waiting for transfers between devices: 31.3 us -> none  [the longest x2 21.1 us: on_device(): lax.all_to_all(roster, 'dw', split_axis=1, concat_axis=1, tiled=True)]
    all_gather x0 -> x2, blocking collectives: none -> 15.5 us  [the longest x1 8.93 us: on_device(): gathered = lax.all_gather(sums, 'dw', axis=0)]
    all_to_all x4 -> x0, starting transfers between devices: 15.4 us -> none  [the longest x2 7.68 us: on_device(): lax.all_to_all(owner_rows, 'dw', split_axis=1, concat_axis=1, tiled=True)]
    dynamic_update_slice x16 -> x0, local copies, waits for them, and re-layouts: 10.5 us -> none  [apply_inverse(): out_blocks = lax.map(one_block, (labels_in, blocks_in))]
  transfers between devices with their start and end apart: 4 -> 2, of which waited for: 3 -> 2; matrix products, arithmetic and copies ran while one was open for 1% -> 0% of each run, Pallas kernels for 0% -> 0%
where the time goes in v1:
time: 60.9 us; the launch traced here: 60.6 us
  Pallas kernels  32.4 us (53%)
  blocking collectives  15.5 us (25%)
  waiting for transfers between devices  4.88 us (8%)
  starting transfers between devices  4.14 us (7%)
  other arithmetic  2.21 us (4%)
  local copies, waits for them, and re-layouts  0.77 us (1%)
  between operations  0.64 us (1%)
    pallas_call x1, Pallas kernels, on_device(): pl.pallas_call(first_kernel, name='first', in_specs=[smem(), vmem(), vmem...  17.6 us
    pallas_call x1, Pallas kernels, on_device(): pl.pallas_call(lambda *refs: last_kernel(inv_root, owned, *refs), name='l...  12.9 us
    all_gather x1, blocking collectives, on_device(): gathered = lax.all_gather(sums, 'dw', axis=0)  8.93 us
    all_gather x1, blocking collectives, on_device(): duals = lax.all_gather(mine, 'dw', axis=0, tiled=True)  6.61 us
    ppermute x2, waiting for transfers between devices, on_device(): lax.ppermute(pack, 'reg', [(i, i ^ stride) for i in range(region_total)])  4.88 us
    ppermute x2, starting transfers between devices, on_device(): lax.ppermute(pack, 'reg', [(i, i ^ stride) for i in range(region_total)])  4.14 us
    pallas_call x1, Pallas kernels, on_device(): pl.pallas_call(lambda *refs: middle_kernel(steps, arch_count, *refs), nam...  1.89 us
  transfers between devices with their start and end apart: 2, of which 2 were waited for; matrix products, arithmetic and copies ran while one was open for 0% of the time, Pallas kernels for 0%

profile of v1, /device:TPU:0, one launch (start us, length us, event | category | flops | bytes accessed | tf_op | source)
XLA Modules:
  0.0 60.6 jit_solution(1986667218197150440)
XLA Ops:
  0.6 0.7 %multiply_bitcast_fusion = f32[16,1]{0,1:T(1,128)S(1)} fusion(s32[16]{0:T(128)} %param.13), kind=kLoop, calls=%fused_computation.1 | loop fusion | flops 32 | bytes 128 | tf_op jit(solution)/shard_map/broadcast_in_dim | solution.py:317
  1.3 0.1 copy.11
  1.4 0.1 pad.2.clone
  1.5 0.8 %maximum_maximum_fusion = f32[16,128]{1,0:T(8,128)S(1)} fusion(f32[16,1]{1,0:T(8,128)S(1)} %copy.11, f32[16,96]{1,0:T(8,128)} %param.14, f32[128]{0:T(128)S(1)} %pad.2.clone), kind=kLoop, calls=%fused_computation | loop fusion | flops 4096 | bytes 14912 | tf_op jit(solution)/shard_map/concatenate | solution.py:316
  2.2 6.6 %all_gather.9.duals_ref.refs_1_.refs_5_ = f32[64,128]{1,0:T(8,128)} all-gather(f32[16,128]{1,0:T(8,128)S(1)} %maximum_maximum_fusion), channel_id=1, replica_groups=mesh['scen'=2,'dw'=4,'reg'=4] {'dw'}, dimensions={0}, use_global_device_ids=true | all-gather | bytes 40960 | tf_op jit(solution)/shard_map/all_gather | solution.py:319
  8.8 17.6 %first.1 = (f32[2560,128]{1,0:T(8,128)}, s32[1,2048]{1,0:T(1,128)}, s32[8,128]{1,0:T(8,128)}, f32[64,384]{1,0:T(8,128)}) custom-call(s32[1,4]{1,0:T(1,128)} %counts_ref.1, s32[1,2048]{1,0:T(1,128)} %bitcast.9, s32[1,2048]{1,0:T(1,128)} %bitcast.10, f32[96,2048]{1,0:T(8,128)} %load_ref.1, f32[64,96,96]{2,1,0:T(8,128)} %refs_9_.1, ...), custom_call_target="tpu_custom_call" | custom-call | tf_op jit(solution)/shard_map/first/pallas_call | solution.py:321
  26.4 8.9 %all-gather = f32[256,384]{1,0:T(8,128)} all-gather(f32[64,384]{1,0:T(8,128)} %get-tuple-element.16), channel_id=2, replica_groups=mesh['scen'=2,'dw'=4,'reg'=4] {'dw'}, dimensions={0}, use_global_device_ids=true | all-gather | bytes 491520 | tf_op jit(solution)/shard_map/all_gather | solution.py:349
  35.3 1.9 %middle.1 = (f32[72,128]{1,0:T(8,128)}, f32[64,128]{1,0:T(8,128)}, f32[64,256]{1,0:T(8,128)}) custom-call(f32[4,64,384]{2,1,0:T(8,128)} %bitcast.8, f32[64,128]{1,0:T(8,128)} %all_gather.9.duals_ref.refs_1_.refs_5_), custom_call_target="tpu_custom_call" | custom-call | tf_op jit(solution)/shard_map/middle/pallas_call | solution.py:350
  37.2 1.6 %collective-permute-start = (f32[72,128]{1,0:T(8,128)}, f32[72,128]{1,0:T(8,128)S(1)}, u32[]{:S(2)}, u32[]{:S(2)}) collective-permute-start(f32[72,128]{1,0:T(8,128)} %get-tuple-element.19), channel_id=1, source_target_pairs={{0,1},{1,0},{2,3},{3,2},{4,5},{5,4},{6,7},{7,6},{8,9},{9,8},{10,11... | collective-permute-start | bytes 110600 | tf_op jit(solution)/shard_map/ppermute | solution.py:367
  38.8 2.6 %collective-permute-done = f32[72,128]{1,0:T(8,128)S(1)} collective-permute-done((f32[72,128]{1,0:T(8,128)}, f32[72,128]{1,0:T(8,128)S(1)}, u32[]{:S(2)}, u32[]{:S(2)}) %collective-permute-start) | collective-permute-done | bytes 36896 | tf_op jit(solution)/shard_map/ppermute | solution.py:367
  41.4 0.8 %add.3.refs_7_ = f32[72,128]{1,0:T(8,128)S(1)} add(f32[72,128]{1,0:T(8,128)} %get-tuple-element.19, f32[72,128]{1,0:T(8,128)S(1)} %collective-permute-done) | non-fusion elementwise | flops 9216 | bytes 110592 | tf_op jit(solution)/shard_map/add | solution.py:366
  42.2 0.0 copy-start
  42.2 2.6 %collective-permute-start.1 = (f32[72,128]{1,0:T(8,128)S(1)}, f32[72,128]{1,0:T(8,128)S(1)}, u32[]{:S(2)}, u32[]{:S(2)}) collective-permute-start(f32[72,128]{1,0:T(8,128)S(1)} %add.3.refs_7_), channel_id=1, source_target_pairs={{0,2},{1,3},{2,0},{3,1},{4,6},{5,7},{6,4},{7,5},{8,10},{9,11},{10,... | collective-permute-start | bytes 110600 | tf_op jit(solution)/shard_map/ppermute | solution.py:367
  44.8 2.3 %collective-permute-done.1.refs_8_ = f32[72,128]{1,0:T(8,128)S(1)} collective-permute-done((f32[72,128]{1,0:T(8,128)S(1)}, f32[72,128]{1,0:T(8,128)S(1)}, u32[]{:S(2)}, u32[]{:S(2)}) %collective-permute-start.1) | collective-permute-done | bytes 36896 | tf_op jit(solution)/shard_map/ppermute | solution.py:367
  47.0 0.0 copy-start.1
  47.0 0.0 copy-done
  47.0 0.6 copy-done.1
  47.7 12.9 %last.1 = (f32[96,2048]{1,0:T(8,128)}, f32[16,96]{1,0:T(8,128)}, f32[1,96]{1,0:T(1,128)}) custom-call(s32[1]{0:T(128)} %bitcast.refs_0_, s32[8,128]{1,0:T(8,128)} %get-tuple-element.13.refs_1_, f32[2560,128]{1,0:T(8,128)} %get-tuple-element.14.refs_2_, s32[1,2048]{1,0:T(1,128)} %get-tuple-element.15.refs_3_, f32[64,128]{1,0:T(8,128)} %get-tuple-element.17.refs_4_, ...), custom_call_target="tpu_custom_call" | custom-call | tf_op jit(solution)/shard_map/last/pallas_call | solution.py:370
  (1 shorter events, 0.0 us)
Async XLA Ops:
  37.2 4.2 %collective-permute-start = (f32[72,128]{1,0:T(8,128)}, f32[72,128]{1,0:T(8,128)S(1)}, u32[]{:S(2)}, u32[]{:S(2)}) collective-permute-start(f32[72,128]{1,0:T(8,128)} %get-tuple-element.19), channel_id=1, source_target_pairs={{0,1},{1,0},{2,3},{3,2},{4,5},{5,4},{6,7},{7,6},{8,9},{9,8},{10,11... | collective-permute-start | bytes 110600 | tf_op jit(solution)/shard_map/ppermute | solution.py:367
  42.2 4.9 %copy-start = (f32[72,128]{1,0:T(8,128)}, f32[72,128]{1,0:T(8,128)S(1)}, u32[]{:S(2)}) copy-start(f32[72,128]{1,0:T(8,128)S(1)} %add.3.refs_7_) | copy-start | bytes 110596
  42.2 4.9 %collective-permute-start.1 = (f32[72,128]{1,0:T(8,128)S(1)}, f32[72,128]{1,0:T(8,128)S(1)}, u32[]{:S(2)}, u32[]{:S(2)}) collective-permute-start(f32[72,128]{1,0:T(8,128)S(1)} %add.3.refs_7_), channel_id=1, source_target_pairs={{0,2},{1,3},{2,0},{3,1},{4,6},{5,7},{6,4},{7,5},{8,10},{9,11},{10,... | collective-permute-start | bytes 110600 | tf_op jit(solution)/shard_map/ppermute | solution.py:367
  47.0 0.6 %copy-start.1 = (f32[72,128]{1,0:T(8,128)}, f32[72,128]{1,0:T(8,128)S(1)}, u32[]{:S(2)}) copy-start(f32[72,128]{1,0:T(8,128)S(1)} %collective-permute-done.1.refs_8_) | copy-start | bytes 110596

commit v2 on v1

v2 whole, which is shorter than its diff:
```python
import math

import jax
import jax.numpy as jnp
from jax import lax
from jax.experimental import pallas as pl
from jax.experimental.pallas import tpu as pltpu
from jax.sharding import PartitionSpec as P

rho_weight = 0.5
dual_rate = 0.1
balance_rate = 1.0

LANES = 128
ROWS = 256
WIN = 48
EXTRA = 32
VMEM_BYTES = 24 * 1024 * 1024

F32 = jnp.float32
BF16 = jnp.bfloat16
NT = (((1,), (1,)), ((), ()))
TN = (((0,), (0,)), ((), ()))


def iota(shape, dim):
    return lax.broadcasted_iota(jnp.int32, shape, dim)


def halves(x):
    high = x.astype(BF16)
    return high, (x - high.astype(F32)).astype(BF16)


def side(x):
    return jnp.concatenate(halves(x), axis=1)


def mm(a, b, dims=None):
    if dims is None:
        return jnp.dot(a, b, preferred_element_type=F32)
    return lax.dot_general(a, b, dims, preferred_element_type=F32)


def fold(x):
    return x[:, :LANES] + x[:, LANES:]


def feeder_hot(rows, steps, count):
    label = jnp.broadcast_to(rows[:, steps : steps + 1], (rows.shape[0], count))
    lane = iota((rows.shape[0], count), 1).astype(F32)
    return jnp.where(label == lane + 1.0, 1.0, 0.0).astype(BF16)


def weights(kkt_ref, a):
    high, low = halves(kkt_ref[a])
    steps = kkt_ref.shape[1]
    gap = jnp.zeros((LANES - steps, steps), BF16)
    return jnp.concatenate([high, gap, low, gap], axis=0)


def apply_matrix(x, matrix):
    count = x.shape[0]
    x = x[:, : matrix.shape[1]]
    rest = x - x.astype(BF16).astype(F32)
    both = mm(jnp.concatenate([x, rest], axis=0).astype(BF16), matrix, NT)
    return both[:count, :LANES] + (both[count:, :LANES] + both[:count, LANES:])


def each_group(offs_ref, arch_count, step):
    for a in range(arch_count):
        step(a, pl.multiple_of(offs_ref[0, a], 8), None)

    @pl.when(offs_ref[2, 0] > WIN)
    def _():
        def group(a, carry):
            start = offs_ref[0, a]
            size = (offs_ref[1, a] + 7) // 8 * 8

            def part(t, inner):
                step(a, pl.multiple_of(start + t * WIN, 8), size - t * WIN)
                return inner

            return lax.fori_loop(1, (size + WIN - 1) // WIN, part, carry)

        lax.fori_loop(0, arch_count, group, 0)


def tiers(most):
    return [t for t in (6, 7, 8) if t < most] + [most]


def put(ref, here, value, limit):
    if limit is not None:
        value = jnp.where(iota((WIN, LANES), 0) < limit, value, ref[here, :])
    ref[here, :] = value


def clear_after(offs_ref, refs):
    for t in range(-(-ROWS // WIN)):
        here = pl.ds(pl.multiple_of(offs_ref[3, 0] + t * WIN, 8), WIN)
        for ref in refs:
            ref[here, :] = jnp.zeros((WIN, LANES), F32)


def sort_kernel(
    counts_hbm, arch_hbm, feeder_hbm, load_hbm,
    xs_ref, pos_ref, offs_ref,
    arch_ref, feeder_ref, load_ref, counts_ref, xt_ref, sems, owned, arch_count,
):
    copies = [
        pltpu.make_async_copy(a, b, sems.at[i])
        for i, (a, b) in enumerate(
            [(arch_hbm, arch_ref), (feeder_hbm, feeder_ref), (load_hbm, load_ref), (counts_hbm, counts_ref)]
        )
    ]
    for copy in copies:
        copy.start()
    steps, rows_count = load_ref.shape
    block_total = counts_ref.shape[1]
    seg = rows_count // block_total
    copies[3].wait()
    copies[0].wait()
    copies[1].wait()
    lane = iota((1, rows_count), 1)
    bound = jnp.zeros((1, rows_count), jnp.int32)
    base = jnp.zeros((1, rows_count), jnp.int32)
    for k in range(block_total):
        inside = lane >= k * seg
        bound = jnp.where(inside, k * seg + counts_ref[0, k], bound)
        base = jnp.where(inside, k * owned, base)
    live = lane < bound
    kind = jnp.where(live, arch_ref[...], -1)
    label = jnp.where(live, lax.rem(feeder_ref[...], owned) + base + 1, 0).astype(F32)

    chunk = 256
    before = jnp.where(iota((chunk, chunk), 0) < iota((chunk, chunk), 1), 1.0, 0.0).astype(BF16)
    arch_iota = iota((arch_count, chunk), 0)
    carry = jnp.zeros((arch_count, 1), F32)
    hots, ranks = [], []
    for c in range(rows_count // chunk):
        hot = jnp.where(kind[:, c * chunk : (c + 1) * chunk] == arch_iota, 1.0, 0.0)
        ranks.append(mm(hot.astype(BF16), before) + carry)
        hots.append(hot)
        carry = carry + jnp.sum(hot, axis=1, keepdims=True)
    eights = jnp.floor((carry + 7.0) * 0.125)
    lower = jnp.where(iota((arch_count, arch_count), 1) < iota((arch_count, arch_count), 0), 1.0, 0.0).astype(BF16)
    offs = mm(lower, jnp.broadcast_to(eights, (arch_count, LANES)).astype(BF16)) * 8.0
    for c in range(rows_count // chunk):
        part = slice(c * chunk, (c + 1) * chunk)
        place = jnp.sum(hots[c] * (ranks[c] + offs[:, :1]), axis=0, keepdims=True)
        pos_ref[:, part] = jnp.where(live[:, part], place, -1.0).astype(jnp.int32)
    diagonal = iota((arch_count, LANES), 0) == iota((arch_count, LANES), 1)
    offs_row = jnp.sum(jnp.where(diagonal, offs, 0.0), axis=0, keepdims=True)
    size_row = jnp.sum(jnp.where(diagonal, jnp.broadcast_to(carry, (arch_count, LANES)), 0.0), axis=0, keepdims=True)
    used = (jnp.sum(eights) * 8.0).astype(jnp.int32)
    blocks = (used + ROWS - 1) // ROWS
    row = iota((8, LANES), 0)
    table = jnp.where(row == 0, offs_row, jnp.where(row == 1, size_row, 0.0)).astype(jnp.int32)
    biggest = jnp.max(carry).astype(jnp.int32)
    offs_ref[...] = jnp.where(row == 2, biggest, jnp.where(row == 3, used, jnp.where(row == 4, blocks, table)))

    copies[2].wait()
    for c in range(rows_count // LANES):
        part = slice(c * LANES, (c + 1) * LANES)
        extra = jnp.where(iota((LANES - steps, LANES), 0) == 0, label[:, part], 0.0)
        block = jnp.concatenate([load_ref[:, part], extra], axis=0).T
        xt_ref[part, :] = side(block)

    def permute(b, inner):
        at = pl.multiple_of(b * ROWS, ROWS)
        total = jnp.zeros((ROWS, 2 * LANES), F32)
        for c in range(rows_count // 512):
            part = slice(c * 512, (c + 1) * 512)
            hot = jnp.where(pos_ref[:, part] - at == iota((ROWS, 512), 0), 1.0, 0.0).astype(BF16)
            total = total + mm(hot, xt_ref[part, :])
        xs_ref[pl.ds(at, ROWS), :] = fold(total)
        return inner

    lax.fori_loop(0, blocks, permute, 0)


def first_kernel(
    block_total, own_ref, cap_ref, offs_vmem, xs_ref, kkt_ref, *rest
):
    piece_refs = rest[:-8]
    y_ref, sums_ref, duals_out, z_ref, r_ref, duals_ref, offs_ref, sem = rest[-8:]
    copy = pltpu.make_async_copy(offs_vmem, offs_ref, sem)
    copy.start()
    arch_count = kkt_ref.shape[0]
    steps = piece_refs[0].shape[1]
    feeders = duals_ref.shape[0]
    owned = feeders // block_total
    own = own_ref[0]
    spare = LANES - steps
    duals_ref[...] = jnp.zeros_like(duals_ref)
    if len(piece_refs) == 1:
        duals_ref[:, 0:steps] = piece_refs[0][...]
    else:
        for p, ref in enumerate(piece_refs):
            duals_ref[pl.ds(pl.multiple_of((own ^ p) * owned, owned), owned), 0:steps] = ref[...]
    duals = duals_ref[...]
    duals_out[...] = duals
    duals_side = side(duals)
    blocks = jnp.max(offs_vmem[4:5, :])

    def pick(b, inner):
        here = pl.ds(pl.multiple_of(b * ROWS, ROWS), ROWS)
        xs = xs_ref[here, :]
        z_ref[here, :] = xs - fold(mm(feeder_hot(xs, steps, feeders), duals_side))
        return inner

    lax.fori_loop(0, blocks, pick, 0)
    copy.wait()

    is_label = iota((WIN, LANES), 1) == steps

    def group(a, row, limit):
        here = pl.ds(row, WIN)
        xs = xs_ref[here, :]
        matrix = weights(kkt_ref, a)
        r = apply_matrix(z_ref[here, :], matrix)
        put(r_ref, here, r, limit)
        y = apply_matrix(xs + rho_weight * r, matrix)
        put(y_ref, here, jnp.where(is_label, xs, y), limit)

    each_group(offs_ref, arch_count, group)
    clear_after(offs_ref, [r_ref, y_ref])

    offs_row = offs_vmem[0:1, :]
    size_row = offs_vmem[1:2, :]

    def gather(b, total):
        at = pl.multiple_of(b * ROWS, ROWS)
        here = pl.ds(at, ROWS)
        row = iota((ROWS, LANES), 0) + at
        member = jnp.where((row >= offs_row) & (row < offs_row + size_row), 1.0, 0.0).astype(BF16)
        y = y_ref[here, :]
        right = jnp.concatenate([*halves(r_ref[here, :]), *halves(y), member], axis=1)
        return total + mm(feeder_hot(y, steps, feeders), right, TN)

    sums = lax.fori_loop(0, blocks, gather, jnp.zeros((feeders, 5 * LANES), F32))
    loads = sums[:, 0:LANES] + sums[:, LANES : 2 * LANES]
    others = sums[:, 2 * LANES : 3 * LANES] + sums[:, 3 * LANES : 4 * LANES]
    counts = sums[:, 4 * LANES :]
    low = jnp.concatenate([counts[:, spare : spare + steps], counts[:, 0:spare]], axis=1)
    high = jnp.concatenate([counts[:, 2 * spare : LANES], counts[:, 0 : 2 * spare]], axis=1)
    lane = iota((feeders, LANES), 1)
    sums_ref[0:feeders, 0:LANES] = jnp.where(lane < steps, loads, low)
    sums_ref[0:feeders, LANES:] = jnp.where(lane < steps, others, high)
    row = iota((8, LANES), 0)
    sums_ref[feeders:, 0:LANES] = jnp.where(row == 0, jnp.sum(loads, axis=0, keepdims=True), 0.0)
    sums_ref[feeders:, LANES:] = jnp.where(row == 0, jnp.sum(others, axis=0, keepdims=True), 0.0)
    mine = pl.ds(pl.multiple_of(own * owned, owned), owned)
    place = iota((owned, LANES), 0)
    cap = jnp.zeros((owned, LANES), jnp.int32)
    for q in range(owned):
        cap = jnp.where(place == q, cap_ref[q], cap)
    cap = jnp.where(iota((owned, LANES), 1) < steps, cap.astype(F32) * 0.001, 0.0)
    sums_ref[mine, 0:LANES] = sums_ref[mine, 0:LANES] - cap


def middle_kernel(steps, arch_count, sums_ref, duals_ref, pack_ref, next_ref, rest_ref):
    total = sums_ref[0]
    for d in range(1, sums_ref.shape[0]):
        total = total + sums_ref[d]
    feeders = duals_ref.shape[0]
    spare = LANES - steps
    excess = total[:feeders, :LANES]
    others = total[:feeders, LANES:]
    lane = iota((feeders, LANES), 1)
    after = jnp.maximum(duals_ref[...] + dual_rate * excess, 0.0)
    after = jnp.where(lane < steps, after, jnp.where(lane == steps, 1.0, 0.0))
    next_ref[...] = after
    counts = jnp.concatenate([excess[:, steps:], others[:, steps:], jnp.zeros((feeders, LANES - 2 * spare), F32)], axis=1)
    rest_ref[:, :LANES] = others
    rest_ref[:, LANES:] = counts
    mixed = lax.dot_general(counts, after, TN, precision=lax.Precision.HIGHEST, preferred_element_type=F32)
    pack_ref[0:arch_count, :] = mixed[:arch_count]
    row = iota((8, LANES), 0)
    pack_ref[arch_count:, :] = jnp.where(
        row == 0, total[feeders : feeders + 1, :LANES], jnp.where(row == 1, total[feeders : feeders + 1, LANES:], 0.0)
    )


def last_kernel(
    inv_root, owned, own_ref, cap_ref, offs_vmem, y_ref, pos_ref, duals_ref, rest_ref, left_ref, right_ref, kkt_ref, target_ref,
    out_ref, feeder_ref, balance_ref,
    z_ref, r_ref, side_ref, acc_ref, target_pad, offs_ref, sem,
):
    copy = pltpu.make_async_copy(offs_vmem, offs_ref, sem)
    copy.start()
    arch_count = kkt_ref.shape[0]
    steps = target_ref.shape[1]
    rows_count = pos_ref.shape[1]
    feeders = duals_ref.shape[0]
    pack = left_ref[...] + right_ref[...]
    target_pad[...] = jnp.zeros_like(target_pad)
    target_pad[0:1, 0:steps] = target_ref[...]
    target = target_pad[0:1, :]
    balance = balance_rate * (pack[arch_count : arch_count + 1] * inv_root - target)
    mixed = pack[:arch_count]
    mixed = mixed + mixed[:, steps : steps + 1] * balance
    duals_all = duals_ref[...] + balance
    duals_side = side(duals_all)
    own = pl.ds(pl.multiple_of(own_ref[0] * owned, owned), owned)
    own_before = duals_ref[own, :]
    own_duals = own_before + balance
    own_rest = rest_ref[own, :]
    blocks = jnp.max(offs_vmem[4:5, :])

    def pick(b, inner):
        here = pl.ds(pl.multiple_of(b * ROWS, ROWS), ROWS)
        z_ref[here, :] = fold(mm(feeder_hot(y_ref[here, :], steps, feeders), duals_side))
        return inner

    lax.fori_loop(0, blocks, pick, 0)
    copy.wait()

    first = iota((EXTRA - owned, LANES), 0) == 0
    acc_ref[...] = jnp.zeros_like(acc_ref)

    def group(a, row, limit):
        here = pl.ds(row, WIN)
        matrix = weights(kkt_ref, a)
        if limit is not None:
            put(r_ref, here, y_ref[here, :] - apply_matrix(z_ref[here, :], matrix), limit)
            return
        rows = own_rest[:, LANES + a : LANES + a + 1] * own_duals
        more = jnp.where(first, mixed[a : a + 1], 0.0)
        done = apply_matrix(jnp.concatenate([z_ref[here, :], rows, more], axis=0), matrix)
        r_ref[here, :] = y_ref[here, :] - done[:WIN]
        acc_ref[...] += done[WIN:]

    each_group(offs_ref, arch_count, group)
    clear_after(offs_ref, [r_ref])
    acc = acc_ref[...]

    loads = own_rest[:, :LANES] - acc[:owned]
    place = iota((owned, LANES), 0)
    cap = jnp.zeros((owned, LANES), jnp.int32)
    for q in range(owned):
        cap = jnp.where(place == q, cap_ref[q], cap)
    after = jnp.maximum(own_before + dual_rate * (loads - cap.astype(F32) * 0.001), 0.0)
    feeder_ref[...] = after[:, :steps]
    system = pack[arch_count + 1 : arch_count + 2] - acc[owned : owned + 1]
    balance_ref[...] = (balance + balance_rate * (system * inv_root - target))[:, :steps]

    def split_rows(b, inner):
        here = pl.ds(pl.multiple_of(b * ROWS, ROWS), ROWS)
        side_ref[here, :] = side(r_ref[here, :])
        return inner

    lax.fori_loop(0, blocks, split_rows, 0)

    def spread(reach):
        def columns(c, inner):
            part = pl.ds(pl.multiple_of(c * 256, 256), 256)
            place = jnp.broadcast_to(pos_ref[:, part].astype(F32), (LANES, 256)).T.astype(jnp.int32)
            hot = jnp.concatenate(
                [
                    jnp.where(place == iota((256, LANES), 1) + q * LANES, 1.0, 0.0).astype(BF16)
                    for q in range(reach * ROWS // LANES)
                ],
                axis=1,
            )
            out_ref[:, part] = fold(mm(hot, side_ref[0 : reach * ROWS, :])).T[:steps]
            return inner

        lax.fori_loop(0, rows_count // 256, columns, 0)

    count = blocks
    low = 0
    for reach in tiers(y_ref.shape[0] // ROWS):
        @pl.when((count > low) & (count <= reach))
        def _():
            def clear(b, inner):
                here = pl.ds(pl.multiple_of(b * ROWS, ROWS), ROWS)
                side_ref[here, :] = jnp.zeros((ROWS, 2 * LANES), BF16)
                return inner

            lax.fori_loop(count, reach, clear, 0)
            spread(reach)

        low = reach


def vmem():
    return pl.BlockSpec(memory_space=pltpu.VMEM)


def smem():
    return pl.BlockSpec(memory_space=pltpu.SMEM)


def hbm():
    return pl.BlockSpec(memory_space=pltpu.HBM)


def stay(x):
    return pltpu.with_memory_space_constraint(x, pltpu.HBM)


def params():
    return pltpu.CompilerParams(vmem_limit_bytes=VMEM_BYTES)


def cost(flops):
    return pl.CostEstimate(flops=flops, transcendentals=0, bytes_accessed=8 * 1024 * 1024)


def exchange(x, axis, mask):
    return lax.ppermute(x, axis, [(i, i ^ mask) for i in range(lax.axis_size(axis))])


def on_device(
    load_base, kkt_inverse, archetype, feeder, live_counts, feeder_cap, dual_start, balance_target
):
    steps, rows_count = load_base.shape
    arch_count = kkt_inverse.shape[0]
    block_total = lax.axis_size("dw")
    region_total = lax.axis_size("reg")
    owned = dual_start.shape[0]
    feeders = owned * block_total
    inv_root = 1.0 / math.sqrt(rows_count * block_total * region_total)
    space = -(-(rows_count + 7 * arch_count + ROWS + WIN) // ROWS) * ROWS
    shape = jax.ShapeDtypeStruct
    own = lax.axis_index("dw").astype(jnp.int32).reshape(1)

    if block_total == 4:
        far = exchange(dual_start, "dw", 2)
    xs, pos, offs = pl.pallas_call(
        lambda *refs: sort_kernel(*refs, owned, arch_count),
        name="sort",
        cost_estimate=cost(5 * 10**9),
        in_specs=[hbm()] * 4,
        out_specs=[vmem()] * 3,
        out_shape=[
            pltpu.VMEM((space, LANES), F32),
            pltpu.VMEM((1, rows_count), jnp.int32),
            pltpu.VMEM((8, LANES), jnp.int32),
        ],
        scratch_shapes=[
            pltpu.VMEM((1, rows_count), jnp.int32),
            pltpu.VMEM((1, rows_count), jnp.int32),
            pltpu.VMEM((steps, rows_count), F32),
            pltpu.SMEM((1, block_total), jnp.int32),
            pltpu.VMEM((rows_count, 2 * LANES), BF16),
            pltpu.SemaphoreType.DMA((4,)),
        ],
        compiler_params=params(),
    )(
        stay(live_counts),
        stay(archetype.reshape(1, rows_count)),
        stay(feeder.reshape(1, rows_count)),
        stay(load_base),
    )
    if block_total == 4:
        far, offs = lax.optimization_barrier((far, offs))
        pieces = [dual_start, exchange(dual_start, "dw", 1), far, exchange(far, "dw", 1)]
    else:
        pieces = [lax.all_gather(dual_start, "dw", axis=0, tiled=True)]
    y, sums, duals = pl.pallas_call(
        lambda *refs: first_kernel(block_total, *refs),
        name="first",
        cost_estimate=cost(6 * 10**9),
        in_specs=[smem()] * 2 + [vmem()] * (3 + len(pieces)),
        out_specs=[vmem()] * 3,
        out_shape=[
            pltpu.VMEM((space, LANES), F32),
            shape((feeders + 8, 2 * LANES), F32),
            pltpu.VMEM((feeders, LANES), F32),
        ],
        scratch_shapes=[
            pltpu.VMEM((space, LANES), F32),
            pltpu.VMEM((space, LANES), F32),
            pltpu.VMEM((feeders, LANES), F32),
            pltpu.SMEM((8, LANES), jnp.int32),
            pltpu.SemaphoreType.DMA,
        ],
        compiler_params=params(),
    )(own, feeder_cap, offs, xs, kkt_inverse, *pieces)
    gathered = lax.all_gather(sums, "dw", axis=0)
    pack, next_duals, rest = pl.pallas_call(
        lambda *refs: middle_kernel(steps, arch_count, *refs),
        name="middle",
        in_specs=[vmem()] * 2,
        out_specs=[vmem()] * 3,
        out_shape=[
            shape((arch_count + 8, LANES), F32),
            shape((feeders, LANES), F32),
            shape((feeders, 2 * LANES), F32),
        ],
        compiler_params=params(),
    )(gathered, duals)
    stride = 1
    other = jnp.zeros_like(pack)
    while stride < region_total:
        if stride > 1:
            pack = pack + other
        other = exchange(pack, "reg", stride)
        stride *= 2
    out, feeder_duals, balance_dual = pl.pallas_call(
        lambda *refs: last_kernel(inv_root, owned, *refs),
        name="last",
        cost_estimate=cost(6 * 10**9),
        in_specs=[smem()] * 2 + [vmem()] * 9,
        out_specs=[vmem()] * 3,
        out_shape=[
            shape((steps, rows_count), F32),
            shape((owned, steps), F32),
            shape((1, steps), F32),
        ],
        scratch_shapes=[
            pltpu.VMEM((space, LANES), F32),
            pltpu.VMEM((space, LANES), F32),
            pltpu.VMEM((space, 2 * LANES), BF16),
            pltpu.VMEM((EXTRA, LANES), F32),
            pltpu.VMEM((8, LANES), F32),
            pltpu.SMEM((8, LANES), jnp.int32),
            pltpu.SemaphoreType.DMA,
        ],
        compiler_params=params(),
    )(
        own, feeder_cap, offs, y, pos, next_duals, rest, pack, other, kkt_inverse,
        balance_target.reshape(1, steps),
    )
    return (out, feeder_duals, balance_dual.reshape(steps))


def solution(mesh):
    in_specs = (
        P(None, ("scen", "dw", "reg")),
        P(),
        P(("scen", "dw", "reg")),
        P(("scen", "dw", "reg")),
        P(("scen", "dw", "reg"), None),
        P(("scen", "dw", "reg")),
        P(("scen", "dw", "reg"), None),
        P("scen"),
    )
    out_specs = (P(None, ("scen", "dw", "reg")), P(("scen", "dw", "reg"), None), P("scen"))
    return jax.shard_map(
        on_device, mesh=mesh, in_specs=in_specs, out_specs=out_specs, check_vma=False
    )
```

time: 60.9 us -> 48.4 us (0.79)
  blocking collectives: 15.5 us -> 5.88 us
  Pallas kernels: 32.4 us -> 26 us
  starting transfers between devices: 4.14 us -> 7.71 us
  other arithmetic: 2.21 us -> 0.01 us
  local copies, waits for them, and re-layouts: 0.77 us -> 2.47 us
    all_gather x1 -> x0, blocking collectives: 6.61 us -> none  [on_device(): duals = lax.all_gather(mine, 'dw', axis=0, tiled=True)]
    ppermute x2 -> x5, starting transfers between devices: 4.14 us -> 7.71 us  [exchange(): lax.ppermute(x, axis, [(i, i ^ mask) for i in range(lax.axis_size(axis))])]
    all_gather x1, blocking collectives: 8.93 us -> 5.88 us  [on_device(): gathered = lax.all_gather(sums, 'dw', axis=0)]
    pallas_call x1 -> x2, Pallas kernels: 17.6 us -> 14.9 us  [the longest x1 9.61 us: on_device(): pl.pallas_call(lambda *refs: first_kernel(block_total, *refs), name='firs...]
    pallas_call x1, Pallas kernels: 12.9 us -> 10.8 us  [on_device(): pl.pallas_call(lambda *refs: last_kernel(inv_root, owned, *refs), name='l...]
    unnamed x4 -> x12, local copies, waits for them, and re-layouts: 0.61 us -> 2.47 us
    pallas_call x1, Pallas kernels: 1.89 us -> 0.33 us  [on_device(): pl.pallas_call(lambda *refs: middle_kernel(steps, arch_count, *refs), nam...]
    concatenate x1 -> x0, other arithmetic: 0.77 us -> none  [on_device(): jnp.concatenate([dual_start, cap[:, None], jnp.zeros((owned, LANES - step...]
  transfers between devices with their start and end apart: 2 -> 5, of which waited for: 2 -> 3; matrix products, arithmetic and copies ran while one was open for 0% -> 0% of each run, Pallas kernels for 0% -> 11%
where the time goes in v2:
time: 48.4 us; the launch traced here: 48.1 us
  Pallas kernels  26 us (54%)
  starting transfers between devices  7.71 us (16%)
  blocking collectives  5.88 us (12%)
  waiting for transfers between devices  5.35 us (11%)
  local copies, waits for them, and re-layouts  2.47 us (5%)
  between operations  0.69 us (1%)
    pallas_call x1, Pallas kernels, on_device(): pl.pallas_call(lambda *refs: last_kernel(inv_root, owned, *refs), name='l...  10.8 us
    pallas_call x1, Pallas kernels, on_device(): pl.pallas_call(lambda *refs: first_kernel(block_total, *refs), name='firs...  9.61 us
    ppermute x5, starting transfers between devices, exchange(): lax.ppermute(x, axis, [(i, i ^ mask) for i in range(lax.axis_size(axis))])  7.71 us
    all_gather x1, blocking collectives, on_device(): gathered = lax.all_gather(sums, 'dw', axis=0)  5.88 us
    ppermute x5, waiting for transfers between devices, exchange(): lax.ppermute(x, axis, [(i, i ^ mask) for i in range(lax.axis_size(axis))])  5.35 us
    pallas_call x1, Pallas kernels, on_device(): pl.pallas_call(lambda *refs: sort_kernel(*refs, owned, arch_count), name=...  5.29 us
    unnamed x12, local copies, waits for them, and re-layouts  2.47 us
  transfers between devices with their start and end apart: 5, of which 3 were waited for; matrix products, arithmetic and copies ran while one was open for 0% of the time, Pallas kernels for 11%

profile of v2, /device:TPU:0, one launch (start us, length us, event | category | flops | bytes accessed | tf_op | source)
XLA Modules:
  0.0 48.1 jit_solution(1191487492389227805)
XLA Ops:
  0.6 3.0 %collective-permute-start = (f32[16,96]{1,0:T(8,128)}, f32[16,96]{1,0:T(8,128)S(1)}, u32[]{:S(2)}, u32[]{:S(2)}) collective-permute-start(f32[16,96]{1,0:T(8,128)} %refs_5_.1), channel_id=1, source_target_pairs={{0,8},{4,12},{8,0},{12,4},{1,9},{5,13},{9,1},{13,5},{2,10},{6,14},... | collective-permute-start | bytes 18440 | tf_op jit(solution)/shard_map/ppermute | solution.py:413
  3.6 0.0 collective-permute-start.1
  3.6 0.0 copy-start
  3.6 0.0 copy-start.1
  3.6 0.0 copy-start.2
  3.6 5.3 %sort.1 = (f32[2816,128]{1,0:T(8,128)S(1)}, s32[1,2048]{1,0:T(1,128)S(1)}, s32[8,128]{1,0:T(8,128)S(1)}) custom-call(s32[1,4]{1,0:T(1,128)} %refs_0_.1, s32[1,2048]{1,0:T(1,128)} %bitcast.8, s32[1,2048]{1,0:T(1,128)} %bitcast.9, f32[96,2048]{1,0:T(8,128)} %refs_3_.1), custom_call_target="tpu_custom_call" | custom-call | flops 5000000000 | bytes 8388608 | tf_op jit(solution)/shard_map/sort/pallas_call | solution.py:432
  8.9 0.0 copy-start.4
  9.0 1.1 %copy-done.4 = f32[2816,128]{1,0:T(8,128)} copy-done((f32[2816,128]{1,0:T(8,128)}, f32[2816,128]{1,0:T(8,128)S(1)}, u32[]{:S(2)}) %copy-start.4) | copy-done | bytes 1441816
  10.1 0.0 collective-permute-done.refs_7_
  10.1 0.1 collective-permute-start.2
  10.1 0.0 collective-permute-done.1.refs_6_
  10.1 1.1 %collective-permute-done.2.refs_8_ = f32[16,96]{1,0:T(8,128)S(1)} collective-permute-done((f32[16,96]{1,0:T(8,128)S(1)}, f32[16,96]{1,0:T(8,128)S(1)}, u32[]{:S(2)}, u32[]{:S(2)}) %collective-permute-start.2) | collective-permute-done | bytes 6176 | tf_op jit(solution)/shard_map/ppermute | solution.py:413
  11.2 0.0 copy-done
  11.2 0.0 copy-done.1
  11.2 0.0 copy-done.2
  11.2 0.0 copy-start.5
  11.3 1.4 %copy-done.5 = f32[2816,128]{1,0:T(8,128)S(1)} copy-done((f32[2816,128]{1,0:T(8,128)S(1)}, f32[2816,128]{1,0:T(8,128)}, u32[]{:S(2)}) %copy-start.5) | copy-done | bytes 1441816
  12.6 0.0 copy-start.3
  12.6 9.6 %first.1 = (f32[2816,128]{1,0:T(8,128)S(1)}, f32[72,256]{1,0:T(8,128)S(1)}, f32[64,128]{1,0:T(8,128)S(1)}) custom-call(s32[1]{0:T(128)} %bitcast.refs_0_, s32[16]{0:T(128)S(1)} %copy-done.2, s32[8,128]{1,0:T(8,128)S(1)} %get-tuple-element.18.refs_2_, f32[2816,128]{1,0:T(8,128)S(1)} %copy-done.5, f32[64,96,96]{2,1,0:T(8,128)S(1)} %copy-done, ...), custom_call_target="tpu_custom_call" | custom-call | flops 6000000000 | bytes 8388608 | tf_op jit(solution)/shard_map/first/pallas_call | solution.py:463
  22.2 5.9 %all-gather = f32[288,256]{1,0:T(8,128)S(1)} all-gather(f32[72,256]{1,0:T(8,128)S(1)} %get-tuple-element.23), channel_id=2, replica_groups=mesh['scen'=2,'dw'=4,'reg'=4] {'dw'}, dimensions={0}, use_global_device_ids=true | all-gather | bytes 368640 | tf_op jit(solution)/shard_map/all_gather | solution.py:483
  28.1 0.3 middle.1
  28.4 1.7 %collective-permute-start.3 = (f32[72,128]{1,0:T(8,128)S(1)}, f32[72,128]{1,0:T(8,128)S(1)}, u32[]{:S(2)}, u32[]{:S(2)}) collective-permute-start(f32[72,128]{1,0:T(8,128)S(1)} %get-tuple-element.27), channel_id=1, source_target_pairs={{0,1},{1,0},{2,3},{3,2},{4,5},{5,4},{6,7},{7,6},{8,9},{9,8},{10,11... | collective-permute-start | bytes 110600 | tf_op jit(solution)/shard_map/ppermute | solution.py:413
  30.2 2.3 %collective-permute-done.3 = f32[72,128]{1,0:T(8,128)S(1)} collective-permute-done((f32[72,128]{1,0:T(8,128)S(1)}, f32[72,128]{1,0:T(8,128)S(1)}, u32[]{:S(2)}, u32[]{:S(2)}) %collective-permute-start.3) | collective-permute-done | bytes 36896 | tf_op jit(solution)/shard_map/ppermute | solution.py:413
  32.5 2.9 %collective-permute-start.4 = (f32[72,128]{1,0:T(8,128)S(1)}, f32[72,128]{1,0:T(8,128)S(1)}, u32[]{:S(2)}, u32[]{:S(2)}) collective-permute-start(f32[72,128]{1,0:T(8,128)S(1)} %add.3.refs_7_), channel_id=1, source_target_pairs={{0,2},{1,3},{2,0},{3,1},{4,6},{5,7},{6,4},{7,5},{8,10},{9,11},{10,... | collective-permute-start | bytes 110600 | tf_op jit(solution)/shard_map/ppermute | solution.py:413
  35.4 1.9 %collective-permute-done.4.refs_8_ = f32[72,128]{1,0:T(8,128)S(1)} collective-permute-done((f32[72,128]{1,0:T(8,128)S(1)}, f32[72,128]{1,0:T(8,128)S(1)}, u32[]{:S(2)}, u32[]{:S(2)}) %collective-permute-start.4) | collective-permute-done | bytes 36896 | tf_op jit(solution)/shard_map/ppermute | solution.py:413
  37.3 0.0 copy-done.3
  37.3 10.8 %last.1 = (f32[96,2048]{1,0:T(8,128)}, f32[16,96]{1,0:T(8,128)}, f32[1,96]{1,0:T(1,128)}) custom-call(s32[1]{0:T(128)} %bitcast.refs_0_, s32[16]{0:T(128)S(1)} %copy-done.2, s32[8,128]{1,0:T(8,128)S(1)} %get-tuple-element.18.refs_2_, f32[2816,128]{1,0:T(8,128)S(1)} %get-tuple-element.21.refs_3_, s32[1,2048]{1,0:T(1,128)S(1)} %get-tuple-element.22.refs_4_, ...), custom_call_target="tpu_custom_call" | custom-call | flops 6000000000 | bytes 8388608 | tf_op jit(solution)/shard_map/last/pallas_call | solution.py:503
  (1 shorter events, 0.0 us)
Async XLA Ops:
  0.6 9.4 %collective-permute-start = (f32[16,96]{1,0:T(8,128)}, f32[16,96]{1,0:T(8,128)S(1)}, u32[]{:S(2)}, u32[]{:S(2)}) collective-permute-start(f32[16,96]{1,0:T(8,128)} %refs_5_.1), channel_id=1, source_target_pairs={{0,8},{4,12},{8,0},{12,4},{1,9},{5,13},{9,1},{13,5},{2,10},{6,14},... | collective-permute-start | bytes 18440 | tf_op jit(solution)/shard_map/ppermute | solution.py:413
  3.6 6.5 %collective-permute-start.1 = (f32[16,96]{1,0:T(8,128)}, f32[16,96]{1,0:T(8,128)S(1)}, u32[]{:S(2)}, u32[]{:S(2)}) collective-permute-start(f32[16,96]{1,0:T(8,128)} %refs_5_.1), channel_id=1, source_target_pairs={{0,4},{4,0},{8,12},{12,8},{1,5},{5,1},{9,13},{13,9},{2,6},{6,2},{1... | collective-permute-start | bytes 18440 | tf_op jit(solution)/shard_map/ppermute | solution.py:413
  3.6 7.6 %copy-start = (f32[64,96,96]{2,1,0:T(8,128)S(1)}, f32[64,96,96]{2,1,0:T(8,128)}, u32[]{:S(2)}) copy-start(f32[64,96,96]{2,1,0:T(8,128)} %refs_9_.1) | copy-start | bytes 7077892
  3.6 7.6 %copy-start.1 = (f32[16,96]{1,0:T(8,128)S(1)}, f32[16,96]{1,0:T(8,128)}, u32[]{:S(2)}) copy-start(f32[16,96]{1,0:T(8,128)} %refs_5_.1) | copy-start | bytes 18436
  3.6 7.6 %copy-start.2 = (s32[16]{0:T(128)S(1)}, s32[16]{0:T(128)}, u32[]{:S(2)}) copy-start(s32[16]{0:T(128)} %refs_1_.3) | copy-start | bytes 196
  8.9 1.1 %copy-start.4 = (f32[2816,128]{1,0:T(8,128)}, f32[2816,128]{1,0:T(8,128)S(1)}, u32[]{:S(2)}) copy-start(f32[2816,128]{1,0:T(8,128)S(1)} %get-tuple-element.19.refs_3_) | copy-start | bytes 4325380
  10.1 1.2 %collective-permute-start.2 = (f32[16,96]{1,0:T(8,128)S(1)}, f32[16,96]{1,0:T(8,128)S(1)}, u32[]{:S(2)}, u32[]{:S(2)}) collective-permute-start(f32[16,96]{1,0:T(8,128)S(1)} %collective-permute-done.refs_7_), channel_id=1, source_target_pairs={{0,4},{4,0},{8,12},{12,8},{1,5},{5,1},{9,13},{13,9},{2,6},{6,2},{1... | collective-permute-start | bytes 18440 | tf_op jit(solution)/shard_map/ppermute | solution.py:413
  11.2 1.4 %copy-start.5 = (f32[2816,128]{1,0:T(8,128)S(1)}, f32[2816,128]{1,0:T(8,128)}, u32[]{:S(2)}) copy-start(f32[2816,128]{1,0:T(8,128)} %copy-done.4) | copy-start | bytes 4325380
  12.6 24.7 %copy-start.3 = (f32[96]{0:T(128)S(1)}, f32[96]{0:T(128)}, u32[]{:S(2)}) copy-start(f32[96]{0:T(128)} %param.15) | copy-start | bytes 1156
  28.4 4.0 %collective-permute-start.3 = (f32[72,128]{1,0:T(8,128)S(1)}, f32[72,128]{1,0:T(8,128)S(1)}, u32[]{:S(2)}, u32[]{:S(2)}) collective-permute-start(f32[72,128]{1,0:T(8,128)S(1)} %get-tuple-element.27), channel_id=1, source_target_pairs={{0,1},{1,0},{2,3},{3,2},{4,5},{5,4},{6,7},{7,6},{8,9},{9,8},{10,11... | collective-permute-start | bytes 110600 | tf_op jit(solution)/shard_map/ppermute | solution.py:413
  32.5 4.9 %collective-permute-start.4 = (f32[72,128]{1,0:T(8,128)S(1)}, f32[72,128]{1,0:T(8,128)S(1)}, u32[]{:S(2)}, u32[]{:S(2)}) collective-permute-start(f32[72,128]{1,0:T(8,128)S(1)} %add.3.refs_7_), channel_id=1, source_target_pairs={{0,2},{1,3},{2,0},{3,1},{4,6},{5,7},{6,4},{7,5},{8,10},{9,11},{10,... | collective-permute-start | bytes 110600 | tf_op jit(solution)/shard_map/ppermute | solution.py:413

commit v3 on v2

--- a/solution.py
+++ b/solution.py
@@ -14,6 +14,7 @@
 LANES = 128
 ROWS = 256
 WIN = 48
+BLOCKS = 8
 EXTRA = 32
 VMEM_BYTES = 24 * 1024 * 1024
 
@@ -97,27 +98,52 @@
 
 
 def clear_after(offs_ref, refs):
-    for t in range(-(-ROWS // WIN)):
-        here = pl.ds(pl.multiple_of(offs_ref[3, 0] + t * WIN, 8), WIN)
-        for ref in refs:
-            ref[here, :] = jnp.zeros((WIN, LANES), F32)
-
-
-def sort_kernel(
-    counts_hbm, arch_hbm, feeder_hbm, load_hbm,
-    xs_ref, pos_ref, offs_ref,
-    arch_ref, feeder_ref, load_ref, counts_ref, xt_ref, sems, owned, arch_count,
+    here = pl.ds(pl.multiple_of(offs_ref[3, 0], 8), WIN)
+    for ref in refs:
+        ref[here, :] = jnp.zeros((WIN, LANES), F32)
+
+
+def each_block(blocks, step, total):
+    for b in range(BLOCKS):
+        total = step(b * ROWS, total)
+
+    def more(b, inner):
+        return step(pl.multiple_of(b * ROWS, ROWS), inner)
+
+    return lax.fori_loop(BLOCKS, blocks, more, total)
+
+
+def cap_column(cap_ref):
+    owned = cap_ref.shape[1]
+    cap = cap_ref[...].astype(F32) * 0.001
+    diagonal = iota((owned, owned), 0) == iota((owned, owned), 1)
+    return jnp.sum(jnp.where(diagonal, cap, 0.0), axis=1, keepdims=True)
+
+
+def first_kernel(
+    counts_hbm, arch_hbm, feeder_hbm, load_hbm, kkt_hbm, start_ref, cap_ref,
+    y_ref, pos_ref, offs_vmem, sums_ref, duals_ref,
+    arch_ref, feeder_ref, load_ref, kkt_ref, counts_ref, xt_ref, code_ref, xs_ref, z_ref, r_ref, mat_ref, offs_ref, sems,
 ):
     copies = [
         pltpu.make_async_copy(a, b, sems.at[i])
         for i, (a, b) in enumerate(
-            [(arch_hbm, arch_ref), (feeder_hbm, feeder_ref), (load_hbm, load_ref), (counts_hbm, counts_ref)]
+            [(arch_hbm, arch_ref), (feeder_hbm, feeder_ref), (load_hbm, load_ref), (counts_hbm, counts_ref), (kkt_hbm, kkt_ref)]
         )
     ]
     for copy in copies:
         copy.start()
-    steps, rows_count = load_ref.shape
+    arch_count, steps, _ = kkt_ref.shape
+    feeders = duals_ref.shape[0]
+    mat_ref[...] = jnp.zeros_like(mat_ref)
+    duals_ref[...] = jnp.zeros_like(duals_ref)
+    duals_ref[:, 0:steps] = start_ref[...]
+    duals_side = side(duals_ref[...])
+    rows_count = load_ref.shape[1]
     block_total = counts_ref.shape[1]
+    owned = feeders // block_total
+    own = lax.axis_index("dw")
+    spare = LANES - steps
     seg = rows_count // block_total
     copies[3].wait()
     copies[0].wait()
@@ -149,7 +175,11 @@
     for c in range(rows_count // chunk):
         part = slice(c * chunk, (c + 1) * chunk)
         place = jnp.sum(hots[c] * (ranks[c] + offs[:, :1]), axis=0, keepdims=True)
-        pos_ref[:, part] = jnp.where(live[:, part], place, -1.0).astype(jnp.int32)
+        place = jnp.where(live[:, part], place, -1.0)
+        pos_ref[:, part] = place.astype(jnp.int32)
+        block = jnp.floor(place * (1.0 / ROWS))
+        within = place - block * ROWS
+        code_ref[:, part] = jnp.where(within == iota((ROWS, chunk), 0).astype(F32), block, -1.0).astype(BF16)
     diagonal = iota((arch_count, LANES), 0) == iota((arch_count, LANES), 1)
     offs_row = jnp.sum(jnp.where(diagonal, offs, 0.0), axis=0, keepdims=True)
     size_row = jnp.sum(jnp.where(diagonal, jnp.broadcast_to(carry, (arch_count, LANES)), 0.0), axis=0, keepdims=True)
@@ -158,7 +188,9 @@
     row = iota((8, LANES), 0)
     table = jnp.where(row == 0, offs_row, jnp.where(row == 1, size_row, 0.0)).astype(jnp.int32)
     biggest = jnp.max(carry).astype(jnp.int32)
-    offs_ref[...] = jnp.where(row == 2, biggest, jnp.where(row == 3, used, jnp.where(row == 4, blocks, table)))
+    offs_vmem[...] = jnp.where(row == 2, biggest, jnp.where(row == 3, used, jnp.where(row == 4, blocks, table)))
+    to_scalar = pltpu.make_async_copy(offs_vmem, offs_ref, sems.at[5])
+    to_scalar.start()
 
     copies[2].wait()
     for c in range(rows_count // LANES):
@@ -167,58 +199,37 @@
         block = jnp.concatenate([load_ref[:, part], extra], axis=0).T
         xt_ref[part, :] = side(block)
 
+    copies[4].wait()
+    for a in range(arch_count):
+        high, low = halves(kkt_ref[a])
+        mat_ref[a, 0:steps, 0:steps] = high
+        mat_ref[a, LANES : LANES + steps, 0:steps] = low
+
     def permute(b, inner):
         at = pl.multiple_of(b * ROWS, ROWS)
-        total = jnp.zeros((ROWS, 2 * LANES), F32)
-        for c in range(rows_count // 512):
-            part = slice(c * 512, (c + 1) * 512)
-            hot = jnp.where(pos_ref[:, part] - at == iota((ROWS, 512), 0), 1.0, 0.0).astype(BF16)
-            total = total + mm(hot, xt_ref[part, :])
-        xs_ref[pl.ds(at, ROWS), :] = fold(total)
+        hot = jnp.where(code_ref[...] == b.astype(F32).astype(BF16), 1.0, 0.0).astype(BF16)
+        xs_ref[pl.ds(at, ROWS), :] = fold(mm(hot, xt_ref[...]))
         return inner
 
     lax.fori_loop(0, blocks, permute, 0)
 
-
-def first_kernel(
-    block_total, own_ref, cap_ref, offs_vmem, xs_ref, kkt_ref, *rest
-):
-    piece_refs = rest[:-8]
-    y_ref, sums_ref, duals_out, z_ref, r_ref, duals_ref, offs_ref, sem = rest[-8:]
-    copy = pltpu.make_async_copy(offs_vmem, offs_ref, sem)
-    copy.start()
-    arch_count = kkt_ref.shape[0]
-    steps = piece_refs[0].shape[1]
-    feeders = duals_ref.shape[0]
-    owned = feeders // block_total
-    own = own_ref[0]
-    spare = LANES - steps
-    duals_ref[...] = jnp.zeros_like(duals_ref)
-    if len(piece_refs) == 1:
-        duals_ref[:, 0:steps] = piece_refs[0][...]
-    else:
-        for p, ref in enumerate(piece_refs):
-            duals_ref[pl.ds(pl.multiple_of((own ^ p) * owned, owned), owned), 0:steps] = ref[...]
-    duals = duals_ref[...]
-    duals_out[...] = duals
-    duals_side = side(duals)
-    blocks = jnp.max(offs_vmem[4:5, :])
-
-    def pick(b, inner):
-        here = pl.ds(pl.multiple_of(b * ROWS, ROWS), ROWS)
+    def pick(at, inner):
+        here = pl.ds(at, ROWS)
         xs = xs_ref[here, :]
         z_ref[here, :] = xs - fold(mm(feeder_hot(xs, steps, feeders), duals_side))
+        r_ref[here, :] = jnp.zeros((ROWS, LANES), F32)
+        y_ref[here, :] = jnp.zeros((ROWS, LANES), F32)
         return inner
 
-    lax.fori_loop(0, blocks, pick, 0)
-    copy.wait()
+    each_block(blocks, pick, 0)
+    to_scalar.wait()
 
     is_label = iota((WIN, LANES), 1) == steps
 
     def group(a, row, limit):
         here = pl.ds(row, WIN)
         xs = xs_ref[here, :]
-        matrix = weights(kkt_ref, a)
+        matrix = mat_ref[a]
         r = apply_matrix(z_ref[here, :], matrix)
         put(r_ref, here, r, limit)
         y = apply_matrix(xs + rho_weight * r, matrix)
@@ -227,19 +238,18 @@
     each_group(offs_ref, arch_count, group)
     clear_after(offs_ref, [r_ref, y_ref])
 
-    offs_row = offs_vmem[0:1, :]
-    size_row = offs_vmem[1:2, :]
-
-    def gather(b, total):
-        at = pl.multiple_of(b * ROWS, ROWS)
+    offs_row = offs_row.astype(jnp.int32)
+    ends_row = offs_row + size_row.astype(jnp.int32)
+
+    def gather(at, total):
         here = pl.ds(at, ROWS)
         row = iota((ROWS, LANES), 0) + at
-        member = jnp.where((row >= offs_row) & (row < offs_row + size_row), 1.0, 0.0).astype(BF16)
+        member = jnp.where((row >= offs_row) & (row < ends_row), 1.0, 0.0).astype(BF16)
         y = y_ref[here, :]
         right = jnp.concatenate([*halves(r_ref[here, :]), *halves(y), member], axis=1)
         return total + mm(feeder_hot(y, steps, feeders), right, TN)
 
-    sums = lax.fori_loop(0, blocks, gather, jnp.zeros((feeders, 5 * LANES), F32))
+    sums = each_block(blocks, gather, jnp.zeros((feeders, 5 * LANES), F32))
     loads = sums[:, 0:LANES] + sums[:, LANES : 2 * LANES]
     others = sums[:, 2 * LANES : 3 * LANES] + sums[:, 3 * LANES : 4 * LANES]
     counts = sums[:, 4 * LANES :]
@@ -252,11 +262,7 @@
     sums_ref[feeders:, 0:LANES] = jnp.where(row == 0, jnp.sum(loads, axis=0, keepdims=True), 0.0)
     sums_ref[feeders:, LANES:] = jnp.where(row == 0, jnp.sum(others, axis=0, keepdims=True), 0.0)
     mine = pl.ds(pl.multiple_of(own * owned, owned), owned)
-    place = iota((owned, LANES), 0)
-    cap = jnp.zeros((owned, LANES), jnp.int32)
-    for q in range(owned):
-        cap = jnp.where(place == q, cap_ref[q], cap)
-    cap = jnp.where(iota((owned, LANES), 1) < steps, cap.astype(F32) * 0.001, 0.0)
+    cap = jnp.where(iota((owned, LANES), 1) < steps, cap_column(cap_ref), 0.0)
     sums_ref[mine, 0:LANES] = sums_ref[mine, 0:LANES] - cap
 
 
@@ -284,13 +290,14 @@
 
 
 def last_kernel(
-    inv_root, owned, own_ref, cap_ref, offs_vmem, y_ref, pos_ref, duals_ref, rest_ref, left_ref, right_ref, kkt_ref, target_ref,
-    out_ref, feeder_ref, balance_ref,
-    z_ref, r_ref, side_ref, acc_ref, target_pad, offs_ref, sem,
+    inv_root, cap_ref, offs_vmem, y_ref, pos_ref, duals_ref, rest_ref, left_ref, right_ref, kkt_ref, target_ref,
+    out_hbm, feeder_ref, balance_ref,
+    z_ref, r_ref, side_ref, acc_ref, target_pad, stage_ref, offs_ref, sem, out_sems,
 ):
     copy = pltpu.make_async_copy(offs_vmem, offs_ref, sem)
     copy.start()
     arch_count = kkt_ref.shape[0]
+    owned = cap_ref.shape[1]
     steps = target_ref.shape[1]
     rows_count = pos_ref.shape[1]
     feeders = duals_ref.shape[0]
@@ -303,18 +310,19 @@
     mixed = mixed + mixed[:, steps : steps + 1] * balance
     duals_all = duals_ref[...] + balance
     duals_side = side(duals_all)
-    own = pl.ds(pl.multiple_of(own_ref[0] * owned, owned), owned)
+    own = pl.ds(pl.multiple_of(lax.axis_index("dw") * owned, owned), owned)
     own_before = duals_ref[own, :]
     own_duals = own_before + balance
     own_rest = rest_ref[own, :]
     blocks = jnp.max(offs_vmem[4:5, :])
 
-    def pick(b, inner):
-        here = pl.ds(pl.multiple_of(b * ROWS, ROWS), ROWS)
+    def pick(at, inner):
+        here = pl.ds(at, ROWS)
         z_ref[here, :] = fold(mm(feeder_hot(y_ref[here, :], steps, feeders), duals_side))
+        r_ref[here, :] = jnp.zeros((ROWS, LANES), F32)
         return inner
 
-    lax.fori_loop(0, blocks, pick, 0)
+    each_block(blocks, pick, 0)
     copy.wait()
 
     first = iota((EXTRA - owned, LANES), 0) == 0
@@ -337,62 +345,52 @@
     acc = acc_ref[...]
 
     loads = own_rest[:, :LANES] - acc[:owned]
-    place = iota((owned, LANES), 0)
-    cap = jnp.zeros((owned, LANES), jnp.int32)
-    for q in range(owned):
-        cap = jnp.where(place == q, cap_ref[q], cap)
-    after = jnp.maximum(own_before + dual_rate * (loads - cap.astype(F32) * 0.001), 0.0)
+    after = jnp.maximum(own_before + dual_rate * (loads - cap_column(cap_ref)), 0.0)
     feeder_ref[...] = after[:, :steps]
     system = pack[arch_count + 1 : arch_count + 2] - acc[owned : owned + 1]
     balance_ref[...] = (balance + balance_rate * (system * inv_root - target))[:, :steps]
 
-    def split_rows(b, inner):
-        here = pl.ds(pl.multiple_of(b * ROWS, ROWS), ROWS)
-        side_ref[here, :] = side(r_ref[here, :])
-        return inner
-
-    lax.fori_loop(0, blocks, split_rows, 0)
+    def columns(c, reach):
+        part = pl.ds(pl.multiple_of(c * ROWS, ROWS), ROWS)
+        place = pos_ref[:, part].astype(F32)
+        block = jnp.floor(place * (1.0 / LANES))
+        within = place - block * LANES
+        code = jnp.where(within == iota((LANES, ROWS), 0).astype(F32), block, -1.0).T.astype(BF16)
+        hot = jnp.concatenate(
+            [jnp.where(code == jnp.bfloat16(q), 1.0, 0.0).astype(BF16) for q in range(reach * ROWS // LANES)], axis=1
+        )
+        stage_ref[:, part] = fold(mm(hot, side_ref[0 : reach * ROWS, :])).T[:steps]
+        return pltpu.make_async_copy(stage_ref.at[:, part], out_hbm.at[:, part], out_sems.at[c])
 
     def spread(reach):
-        def columns(c, inner):
-            part = pl.ds(pl.multiple_of(c * 256, 256), 256)
-            place = jnp.broadcast_to(pos_ref[:, part].astype(F32), (LANES, 256)).T.astype(jnp.int32)
-            hot = jnp.concatenate(
-                [
-                    jnp.where(place == iota((256, LANES), 1) + q * LANES, 1.0, 0.0).astype(BF16)
-                    for q in range(reach * ROWS // LANES)
-                ],
-                axis=1,
-            )
-            out_ref[:, part] = fold(mm(hot, side_ref[0 : reach * ROWS, :])).T[:steps]
+        def pair(c, inner):
+            for half in range(2):
+                columns(2 * c + half, reach).start()
             return inner
 
-        lax.fori_loop(0, rows_count // 256, columns, 0)
+        lax.fori_loop(0, rows_count // (2 * ROWS), pair, 0)
 
     count = blocks
     low = 0
     for reach in tiers(y_ref.shape[0] // ROWS):
         @pl.when((count > low) & (count <= reach))
         def _():
-            def clear(b, inner):
-                here = pl.ds(pl.multiple_of(b * ROWS, ROWS), ROWS)
-                side_ref[here, :] = jnp.zeros((ROWS, 2 * LANES), BF16)
-                return inner
-
-            lax.fori_loop(count, reach, clear, 0)
+            for b in range(reach):
+                here = slice(b * ROWS, (b + 1) * ROWS)
+                side_ref[here, :] = side(r_ref[here, :])
             spread(reach)
 
         low = reach
+
+    for c in range(rows_count // ROWS):
+        part = slice(c * ROWS, (c + 1) * ROWS)
+        pltpu.make_async_copy(stage_ref.at[:, part], out_hbm.at[:, part], out_sems.at[c]).wait()
 
 
 def vmem():
     return pl.BlockSpec(memory_space=pltpu.VMEM)
 
 
-def smem():
-    return pl.BlockSpec(memory_space=pltpu.SMEM)
-
-
 def hbm():
     return pl.BlockSpec(memory_space=pltpu.HBM)
 
@@ -403,10 +401,6 @@
 
 def params():
     return pltpu.CompilerParams(vmem_limit_bytes=VMEM_BYTES)
-
-
-def cost(flops):
-    return pl.CostEstimate(flops=flops, transcendentals=0, bytes_accessed=8 * 1024 * 1024)
 
 
 def exchange(x, axis, mask):
@@ -425,28 +419,34 @@
     inv_root = 1.0 / math.sqrt(rows_count * block_total * region_total)
     space = -(-(rows_count + 7 * arch_count + ROWS + WIN) // ROWS) * ROWS
     shape = jax.ShapeDtypeStruct
-    own = lax.axis_index("dw").astype(jnp.int32).reshape(1)
-
-    if block_total == 4:
-        far = exchange(dual_start, "dw", 2)
-    xs, pos, offs = pl.pallas_call(
-        lambda *refs: sort_kernel(*refs, owned, arch_count),
-        name="sort",
-        cost_estimate=cost(5 * 10**9),
-        in_specs=[hbm()] * 4,
-        out_specs=[vmem()] * 3,
+    cap = feeder_cap.reshape(1, owned)
+    duals = lax.all_gather(dual_start, "dw", axis=0, tiled=True)
+    y, pos, offs, sums, duals = pl.pallas_call(
+        first_kernel,
+        name="first",
+        in_specs=[hbm()] * 5 + [vmem()] * 2,
+        out_specs=[vmem()] * 5,
         out_shape=[
-            pltpu.VMEM((space, LANES), F32),
-            pltpu.VMEM((1, rows_count), jnp.int32),
-            pltpu.VMEM((8, LANES), jnp.int32),
+            shape((space, LANES), F32),
+            shape((1, rows_count), jnp.int32),
+            shape((8, LANES), jnp.int32),
+            shape((feeders + 8, 2 * LANES), F32),
+            shape((feeders, LANES), F32),
         ],
         scratch_shapes=[
             pltpu.VMEM((1, rows_count), jnp.int32),
             pltpu.VMEM((1, rows_count), jnp.int32),
             pltpu.VMEM((steps, rows_count), F32),
+            pltpu.VMEM((arch_count, steps, steps), F32),
             pltpu.SMEM((1, block_total), jnp.int32),
             pltpu.VMEM((rows_count, 2 * LANES), BF16),
-            pltpu.SemaphoreType.DMA((4,)),
+            pltpu.VMEM((ROWS, rows_count), BF16),
+            pltpu.VMEM((space, LANES), F32),
+            pltpu.VMEM((space, LANES), F32),
+            pltpu.VMEM((space, LANES), F32),
+            pltpu.VMEM((arch_count, 2 * LANES, LANES), BF16),
+            pltpu.SMEM((8, LANES), jnp.int32),
+            pltpu.SemaphoreType.DMA((6,)),
         ],
         compiler_params=params(),
     )(
@@ -454,32 +454,10 @@
         stay(archetype.reshape(1, rows_count)),
         stay(feeder.reshape(1, rows_count)),
         stay(load_base),
+        stay(kkt_inverse),
+        duals,
+        cap,
     )
-    if block_total == 4:
-        far, offs = lax.optimization_barrier((far, offs))
-        pieces = [dual_start, exchange(dual_start, "dw", 1), far, exchange(far, "dw", 1)]
-    else:
-        pieces = [lax.all_gather(dual_start, "dw", axis=0, tiled=True)]
-    y, sums, duals = pl.pallas_call(
-        lambda *refs: first_kernel(block_total, *refs),
-        name="first",
-        cost_estimate=cost(6 * 10**9),
-        in_specs=[smem()] * 2 + [vmem()] * (3 + len(pieces)),
-        out_specs=[vmem()] * 3,
-        out_shape=[
-            pltpu.VMEM((space, LANES), F32),
-            shape((feeders + 8, 2 * LANES), F32),
-            pltpu.VMEM((feeders, LANES), F32),
-        ],
-        scratch_shapes=[
-            pltpu.VMEM((space, LANES), F32),
-            pltpu.VMEM((space, LANES), F32),
-            pltpu.VMEM((feeders, LANES), F32),
-            pltpu.SMEM((8, LANES), jnp.int32),
-            pltpu.SemaphoreType.DMA,
-        ],
-        compiler_params=params(),
-    )(own, feeder_cap, offs, xs, kkt_inverse, *pieces)
     gathered = lax.all_gather(sums, "dw", axis=0)
     pack, next_duals, rest = pl.pallas_call(
         lambda *refs: middle_kernel(steps, arch_count, *refs),
@@ -501,11 +479,10 @@
         other = exchange(pack, "reg", stride)
         stride *= 2
     out, feeder_duals, balance_dual = pl.pallas_call(
-        lambda *refs: last_kernel(inv_root, owned, *refs),
+        lambda *refs: last_kernel(inv_root, *refs),
         name="last",
-        cost_estimate=cost(6 * 10**9),
-        in_specs=[smem()] * 2 + [vmem()] * 9,
-        out_specs=[vmem()] * 3,
+        in_specs=[vmem()] * 10,
+        out_specs=[hbm()] + [vmem()] * 2,
         out_shape=[
             shape((steps, rows_count), F32),
             shape((owned, steps), F32),
@@ -517,12 +494,14 @@
             pltpu.VMEM((space, 2 * LANES), BF16),
             pltpu.VMEM((EXTRA, LANES), F32),
             pltpu.VMEM((8, LANES), F32),
+            pltpu.VMEM((steps, rows_count), F32),
             pltpu.SMEM((8, LANES), jnp.int32),
             pltpu.SemaphoreType.DMA,
+            pltpu.SemaphoreType.DMA((rows_count // ROWS,)),
         ],
         compiler_params=params(),
     )(
-        own, feeder_cap, offs, y, pos, next_duals, rest, pack, other, kkt_inverse,
+        cap, offs, y, pos, next_duals, rest, pack, other, kkt_inverse,
         balance_target.reshape(1, steps),
     )
     return (out, feeder_duals, balance_dual.reshape(steps))

time: 48.4 us -> 43.9 us (0.907)
  blocking collectives: 5.88 us -> 13 us
  Pallas kernels: 26 us -> 20 us
  starting transfers between devices: 7.71 us -> 4.63 us
  local copies, waits for them, and re-layouts: 2.47 us -> 0.67 us
  waiting for transfers between devices: 5.35 us -> 4.38 us
    all_gather x0 -> x1, blocking collectives: none -> 6.52 us  [on_device(): duals = lax.all_gather(dual_start, 'dw', axis=0, tiled=True)]
    pallas_call x3 -> x2, Pallas kernels: 25.7 us -> 19.7 us  [the longest x1 10.6 us: on_device(): pl.pallas_call(first_kernel, name='first', in_specs=[hbm()] * 5 + [vmem()...]
    ppermute x5 -> x2, starting transfers between devices: 7.71 us -> 4.63 us  [exchange(): lax.ppermute(x, axis, [(i, i ^ mask) for i in range(lax.axis_size(axis))])]
    unnamed x12 -> x8, local copies, waits for them, and re-layouts: 2.47 us -> 0.67 us
    ppermute x5 -> x2, waiting for transfers between devices: 5.35 us -> 4.38 us  [exchange(): lax.ppermute(x, axis, [(i, i ^ mask) for i in range(lax.axis_size(axis))])]
    all_gather x1, blocking collectives: 5.88 us -> 6.45 us  [on_device(): gathered = lax.all_gather(sums, 'dw', axis=0)]
  transfers between devices with their start and end apart: 5 -> 2, of which waited for: 3 -> 2; matrix products, arithmetic and copies ran while one was open for 0% -> 0% of each run, Pallas kernels for 11% -> 0%
where the time goes in v3:
time: 43.9 us; the launch traced here: 43.5 us
  Pallas kernels  20 us (46%)
  blocking collectives  13 us (30%)
  starting transfers between devices  4.63 us (11%)
  waiting for transfers between devices  4.38 us (10%)
  between operations  0.82 us (2%)
  local copies, waits for them, and re-layouts  0.67 us (2%)
    pallas_call x1, Pallas kernels, on_device(): pl.pallas_call(first_kernel, name='first', in_specs=[hbm()] * 5 + [vmem()...  10.6 us
    pallas_call x1, Pallas kernels, on_device(): pl.pallas_call(lambda *refs: last_kernel(inv_root, *refs), name='last', i...  9.1 us
    all_gather x1, blocking collectives, on_device(): duals = lax.all_gather(dual_start, 'dw', axis=0, tiled=True)  6.52 us
    all_gather x1, blocking collectives, on_device(): gathered = lax.all_gather(sums, 'dw', axis=0)  6.45 us
    ppermute x2, starting transfers between devices, exchange(): lax.ppermute(x, axis, [(i, i ^ mask) for i in range(lax.axis_size(axis))])  4.63 us
    ppermute x2, waiting for transfers between devices, exchange(): lax.ppermute(x, axis, [(i, i ^ mask) for i in range(lax.axis_size(axis))])  4.38 us
  transfers between devices with their start and end apart: 2, of which 2 were waited for; matrix products, arithmetic and copies ran while one was open for 0% of the time, Pallas kernels for 0%

profile of v3, /device:TPU:0, one launch (start us, length us, event | category | flops | bytes accessed | tf_op | source)
XLA Modules:
  0.0 43.5 jit_solution(9685572353696857696)
XLA Ops:
  0.6 0.0 copy-start
  0.6 6.5 %all_gather.9.start_ref = f32[64,96]{1,0:T(8,128)S(1)} all-gather(f32[16,96]{1,0:T(8,128)} %param.14), channel_id=1, replica_groups=mesh['scen'=2,'dw'=4,'reg'=4] {'dw'}, dimensions={0}, use_global_device_ids=true | all-gather | bytes 30720 | tf_op jit(solution)/shard_map/all_gather | solution.py:423
  7.2 0.0 copy-start.1
  7.2 0.7 %copy-done.1 = s32[16]{0:T(128)S(1)} copy-done((s32[16]{0:T(128)S(1)}, s32[16]{0:T(128)}, u32[]{:S(2)}) %copy-start.1) | copy-done | bytes 88
  7.8 0.0 copy-start.2
  7.8 0.0 copy-start.3
  7.8 10.6 %first.1 = (f32[2816,128]{1,0:T(8,128)S(1)}, s32[1,2048]{1,0:T(1,128)S(1)}, s32[8,128]{1,0:T(8,128)S(1)}, f32[72,256]{1,0:T(8,128)S(1)}, f32[64,128]{1,0:T(8,128)S(1)}) custom-call(s32[1,4]{1,0:T(1,128)} %counts_hbm.1, s32[1,2048]{1,0:T(1,128)} %bitcast.10, s32[1,2048]{1,0:T(1,128)} %bitcast.11, f32[96,2048]{1,0:T(8,128)} %load_hbm.1, ...), custom_call_target="tpu_custom_call" | custom-call | tf_op jit(solution)/shard_map/first/pallas_call | solution.py:424
  18.4 6.4 %all-gather = f32[288,256]{1,0:T(8,128)S(1)} all-gather(f32[72,256]{1,0:T(8,128)S(1)} %get-tuple-element.17), channel_id=2, replica_groups=mesh['scen'=2,'dw'=4,'reg'=4] {'dw'}, dimensions={0}, use_global_device_ids=true | all-gather | bytes 368640 | tf_op jit(solution)/shard_map/all_gather | solution.py:461
  24.9 0.3 middle.1
  25.2 1.6 %collective-permute-start = (f32[72,128]{1,0:T(8,128)S(1)}, f32[72,128]{1,0:T(8,128)S(1)}, u32[]{:S(2)}, u32[]{:S(2)}) collective-permute-start(f32[72,128]{1,0:T(8,128)S(1)} %get-tuple-element.21), channel_id=1, source_target_pairs={{0,1},{1,0},{2,3},{3,2},{4,5},{5,4},{6,7},{7,6},{8,9},{9,8},{10,11... | collective-permute-start | bytes 110600 | tf_op jit(solution)/shard_map/ppermute | solution.py:407
  26.8 2.4 %collective-permute-done = f32[72,128]{1,0:T(8,128)S(1)} collective-permute-done((f32[72,128]{1,0:T(8,128)S(1)}, f32[72,128]{1,0:T(8,128)S(1)}, u32[]{:S(2)}, u32[]{:S(2)}) %collective-permute-start) | collective-permute-done | bytes 36896 | tf_op jit(solution)/shard_map/ppermute | solution.py:407
  29.3 3.1 %collective-permute-start.1 = (f32[72,128]{1,0:T(8,128)S(1)}, f32[72,128]{1,0:T(8,128)S(1)}, u32[]{:S(2)}, u32[]{:S(2)}) collective-permute-start(f32[72,128]{1,0:T(8,128)S(1)} %add.3.refs_6_), channel_id=1, source_target_pairs={{0,2},{1,3},{2,0},{3,1},{4,6},{5,7},{6,4},{7,5},{8,10},{9,11},{10,... | collective-permute-start | bytes 110600 | tf_op jit(solution)/shard_map/ppermute | solution.py:407
  32.3 1.9 %collective-permute-done.1.refs_7_ = f32[72,128]{1,0:T(8,128)S(1)} collective-permute-done((f32[72,128]{1,0:T(8,128)S(1)}, f32[72,128]{1,0:T(8,128)S(1)}, u32[]{:S(2)}, u32[]{:S(2)}) %collective-permute-start.1) | collective-permute-done | bytes 36896 | tf_op jit(solution)/shard_map/ppermute | solution.py:407
  34.2 0.0 copy-done
  34.2 0.0 copy-done.2
  34.2 0.0 copy-done.3
  34.3 9.1 %last.1 = (f32[96,2048]{1,0:T(8,128)}, f32[16,96]{1,0:T(8,128)}, f32[1,96]{1,0:T(1,128)}) custom-call(s32[1,16]{1,0:T(1,128)S(1)} %bitcast.8, s32[8,128]{1,0:T(8,128)S(1)} %get-tuple-element.14.refs_1_, f32[2816,128]{1,0:T(8,128)S(1)} %get-tuple-element.15.refs_2_, s32[1,2048]{1,0:T(1,128)S(1)} %get-tuple-element.16.refs_3_, ...), custom_call_target="tpu_custom_call" | custom-call | tf_op jit(solution)/shard_map/last/pallas_call | solution.py:481
  (1 shorter events, 0.0 us)
Async XLA Ops:
  0.6 33.6 %copy-start = (f32[64,96,96]{2,1,0:T(8,128)S(1)}, f32[64,96,96]{2,1,0:T(8,128)}, u32[]{:S(2)}) copy-start(f32[64,96,96]{2,1,0:T(8,128)} %refs_8_.1) | copy-start | bytes 7077892
  7.2 0.7 %copy-start.1 = (s32[16]{0:T(128)S(1)}, s32[16]{0:T(128)}, u32[]{:S(2)}) copy-start(s32[16]{0:T(128)} %param.13) | copy-start | bytes 196
  7.8 26.4 %copy-start.2 = (s32[16]{0:T(128)S(1)}, s32[16]{0:T(128)}, u32[]{:S(2)}) copy-start(s32[16]{0:T(128)} %param.13) | copy-start | bytes 196
  7.8 26.4 %copy-start.3 = (f32[96]{0:T(128)S(1)}, f32[96]{0:T(128)}, u32[]{:S(2)}) copy-start(f32[96]{0:T(128)} %param.15) | copy-start | bytes 1156
  25.2 4.0 %collective-permute-start = (f32[72,128]{1,0:T(8,128)S(1)}, f32[72,128]{1,0:T(8,128)S(1)}, u32[]{:S(2)}, u32[]{:S(2)}) collective-permute-start(f32[72,128]{1,0:T(8,128)S(1)} %get-tuple-element.21), channel_id=1, source_target_pairs={{0,1},{1,0},{2,3},{3,2},{4,5},{5,4},{6,7},{7,6},{8,9},{9,8},{10,11... | collective-permute-start | bytes 110600 | tf_op jit(solution)/shard_map/ppermute | solution.py:407
  29.3 5.0 %collective-permute-start.1 = (f32[72,128]{1,0:T(8,128)S(1)}, f32[72,128]{1,0:T(8,128)S(1)}, u32[]{:S(2)}, u32[]{:S(2)}) collective-permute-start(f32[72,128]{1,0:T(8,128)S(1)} %add.3.refs_6_), channel_id=1, source_target_pairs={{0,2},{1,3},{2,0},{3,1},{4,6},{5,7},{6,4},{7,5},{8,10},{9,11},{10,... | collective-permute-start | bytes 110600 | tf_op jit(solution)/shard_map/ppermute | solution.py:407

commit v4 on v3

--- a/solution.py
+++ b/solution.py
@@ -53,11 +53,18 @@
     return jnp.where(label == lane + 1.0, 1.0, 0.0).astype(BF16)
 
 
-def weights(kkt_ref, a):
-    high, low = halves(kkt_ref[a])
-    steps = kkt_ref.shape[1]
-    gap = jnp.zeros((LANES - steps, steps), BF16)
-    return jnp.concatenate([high, gap, low, gap], axis=0)
+def split_matrices(kkt_ref, mat_ref):
+    arch_count, steps, _ = kkt_ref.shape
+    for a in range(arch_count):
+        high, low = halves(kkt_ref[a])
+        mat_ref[a, 0:steps, 0:steps] = high
+        mat_ref[a, LANES : LANES + steps, 0:steps] = low
+
+
+def row_code(place):
+    block = jnp.floor(place * (1.0 / ROWS))
+    within = place - block * ROWS
+    return jnp.where(within == iota((ROWS, place.shape[1]), 0).astype(F32), block, -1.0).astype(BF16)
 
 
 def apply_matrix(x, matrix):
@@ -120,34 +127,20 @@
     return jnp.sum(jnp.where(diagonal, cap, 0.0), axis=1, keepdims=True)
 
 
-def first_kernel(
-    counts_hbm, arch_hbm, feeder_hbm, load_hbm, kkt_hbm, start_ref, cap_ref,
-    y_ref, pos_ref, offs_vmem, sums_ref, duals_ref,
-    arch_ref, feeder_ref, load_ref, kkt_ref, counts_ref, xt_ref, code_ref, xs_ref, z_ref, r_ref, mat_ref, offs_ref, sems,
+def rank_kernel(
+    owned, arch_count, counts_hbm, arch_hbm, feeder_hbm, pos_ref, label_ref, offs_ref, counts_ref, arch_ref, feeder_ref, sems
 ):
     copies = [
         pltpu.make_async_copy(a, b, sems.at[i])
-        for i, (a, b) in enumerate(
-            [(arch_hbm, arch_ref), (feeder_hbm, feeder_ref), (load_hbm, load_ref), (counts_hbm, counts_ref), (kkt_hbm, kkt_ref)]
-        )
+        for i, (a, b) in enumerate([(counts_hbm, counts_ref), (arch_hbm, arch_ref), (feeder_hbm, feeder_ref)])
     ]
     for copy in copies:
         copy.start()
-    arch_count, steps, _ = kkt_ref.shape
-    feeders = duals_ref.shape[0]
-    mat_ref[...] = jnp.zeros_like(mat_ref)
-    duals_ref[...] = jnp.zeros_like(duals_ref)
-    duals_ref[:, 0:steps] = start_ref[...]
-    duals_side = side(duals_ref[...])
-    rows_count = load_ref.shape[1]
+    rows_count = arch_ref.shape[1]
     block_total = counts_ref.shape[1]
-    owned = feeders // block_total
-    own = lax.axis_index("dw")
-    spare = LANES - steps
     seg = rows_count // block_total
-    copies[3].wait()
-    copies[0].wait()
-    copies[1].wait()
+    for copy in copies:
+        copy.wait()
     lane = iota((1, rows_count), 1)
     bound = jnp.zeros((1, rows_count), jnp.int32)
     base = jnp.zeros((1, rows_count), jnp.int32)
@@ -157,7 +150,7 @@
         base = jnp.where(inside, k * owned, base)
     live = lane < bound
     kind = jnp.where(live, arch_ref[...], -1)
-    label = jnp.where(live, lax.rem(feeder_ref[...], owned) + base + 1, 0).astype(F32)
+    label_ref[...] = jnp.where(live, lax.rem(feeder_ref[...], owned) + base + 1, 0).astype(F32)
 
     chunk = 256
     before = jnp.where(iota((chunk, chunk), 0) < iota((chunk, chunk), 1), 1.0, 0.0).astype(BF16)
@@ -177,9 +170,6 @@
         place = jnp.sum(hots[c] * (ranks[c] + offs[:, :1]), axis=0, keepdims=True)
         place = jnp.where(live[:, part], place, -1.0)
         pos_ref[:, part] = place.astype(jnp.int32)
-        block = jnp.floor(place * (1.0 / ROWS))
-        within = place - block * ROWS
-        code_ref[:, part] = jnp.where(within == iota((ROWS, chunk), 0).astype(F32), block, -1.0).astype(BF16)
     diagonal = iota((arch_count, LANES), 0) == iota((arch_count, LANES), 1)
     offs_row = jnp.sum(jnp.where(diagonal, offs, 0.0), axis=0, keepdims=True)
     size_row = jnp.sum(jnp.where(diagonal, jnp.broadcast_to(carry, (arch_count, LANES)), 0.0), axis=0, keepdims=True)
@@ -188,22 +178,55 @@
     row = iota((8, LANES), 0)
     table = jnp.where(row == 0, offs_row, jnp.where(row == 1, size_row, 0.0)).astype(jnp.int32)
     biggest = jnp.max(carry).astype(jnp.int32)
-    offs_vmem[...] = jnp.where(row == 2, biggest, jnp.where(row == 3, used, jnp.where(row == 4, blocks, table)))
-    to_scalar = pltpu.make_async_copy(offs_vmem, offs_ref, sems.at[5])
-    to_scalar.start()
-
-    copies[2].wait()
+    offs_ref[...] = jnp.where(row == 2, biggest, jnp.where(row == 3, used, jnp.where(row == 4, blocks, table)))
+
+
+def first_kernel(block_total, load_hbm, kkt_hbm, start_hbm, cap_hbm, pos_ref, label_ref, offs_vmem, *rest):
+    piece_refs = rest[:-15]
+    y_ref, sums_ref, duals_ref, load_ref, kkt_ref, start_ref, cap_ref, xt_ref, code_ref, xs_ref, z_ref, r_ref, mat_ref, offs_ref, sems = rest[-15:]
+    copies = [
+        pltpu.make_async_copy(a, b, sems.at[i])
+        for i, (a, b) in enumerate([
+                (load_hbm, load_ref),
+                (kkt_hbm, kkt_ref),
+                (offs_vmem, offs_ref),
+                (start_hbm, start_ref),
+                (cap_hbm, cap_ref),
+            ])
+    ]
+    for copy in copies:
+        copy.start()
+    arch_count, steps, _ = kkt_ref.shape
+    rows_count = load_ref.shape[1]
+    feeders = duals_ref.shape[0]
+    owned = feeders // block_total
+    own = lax.axis_index("dw")
+    spare = LANES - steps
+    label = label_ref[...]
+    blocks = jnp.max(offs_vmem[4:5, :])
+    mat_ref[...] = jnp.zeros_like(mat_ref)
+    for c in range(rows_count // ROWS):
+        part = slice(c * ROWS, (c + 1) * ROWS)
+        code_ref[:, part] = row_code(pos_ref[:, part].astype(F32))
+
+    copies[3].wait()
+    copies[4].wait()
+    duals_ref[...] = jnp.zeros_like(duals_ref)
+    if len(piece_refs) == 1:
+        duals_ref[:, 0:steps] = piece_refs[0][...]
+    else:
+        for p, ref in enumerate([start_ref, *piece_refs]):
+            duals_ref[pl.ds(pl.multiple_of((own ^ p) * owned, owned), owned), 0:steps] = ref[...]
+    duals_side = side(duals_ref[...])
+    copies[0].wait()
     for c in range(rows_count // LANES):
         part = slice(c * LANES, (c + 1) * LANES)
         extra = jnp.where(iota((LANES - steps, LANES), 0) == 0, label[:, part], 0.0)
         block = jnp.concatenate([load_ref[:, part], extra], axis=0).T
         xt_ref[part, :] = side(block)
 
-    copies[4].wait()
-    for a in range(arch_count):
-        high, low = halves(kkt_ref[a])
-        mat_ref[a, 0:steps, 0:steps] = high
-        mat_ref[a, LANES : LANES + steps, 0:steps] = low
+    copies[1].wait()
+    split_matrices(kkt_ref, mat_ref)
 
     def permute(b, inner):
         at = pl.multiple_of(b * ROWS, ROWS)
@@ -222,7 +245,7 @@
         return inner
 
     each_block(blocks, pick, 0)
-    to_scalar.wait()
+    copies[2].wait()
 
     is_label = iota((WIN, LANES), 1) == steps
 
@@ -238,8 +261,8 @@
     each_group(offs_ref, arch_count, group)
     clear_after(offs_ref, [r_ref, y_ref])
 
-    offs_row = offs_row.astype(jnp.int32)
-    ends_row = offs_row + size_row.astype(jnp.int32)
+    offs_row = offs_vmem[0:1, :]
+    ends_row = offs_row + offs_vmem[1:2, :]
 
     def gather(at, total):
         here = pl.ds(at, ROWS)
@@ -292,7 +315,7 @@
 def last_kernel(
     inv_root, cap_ref, offs_vmem, y_ref, pos_ref, duals_ref, rest_ref, left_ref, right_ref, kkt_ref, target_ref,
     out_hbm, feeder_ref, balance_ref,
-    z_ref, r_ref, side_ref, acc_ref, target_pad, stage_ref, offs_ref, sem, out_sems,
+    z_ref, r_ref, side_ref, mat_ref, code_ref, acc_ref, target_pad, stage_ref, offs_ref, sem, out_sems,
 ):
     copy = pltpu.make_async_copy(offs_vmem, offs_ref, sem)
     copy.start()
@@ -323,6 +346,11 @@
         return inner
 
     each_block(blocks, pick, 0)
+    mat_ref[...] = jnp.zeros_like(mat_ref)
+    split_matrices(kkt_ref, mat_ref)
+    for c in range(rows_count // ROWS):
+        part = slice(c * ROWS, (c + 1) * ROWS)
+        code_ref[:, part] = row_code(pos_ref[:, part].astype(F32))
     copy.wait()
 
     first = iota((EXTRA - owned, LANES), 0) == 0
@@ -330,7 +358,7 @@
 
     def group(a, row, limit):
         here = pl.ds(row, WIN)
-        matrix = weights(kkt_ref, a)
+        matrix = mat_ref[a]
         if limit is not None:
             put(r_ref, here, y_ref[here, :] - apply_matrix(z_ref[here, :], matrix), limit)
             return
@@ -352,14 +380,10 @@
 
     def columns(c, reach):
         part = pl.ds(pl.multiple_of(c * ROWS, ROWS), ROWS)
-        place = pos_ref[:, part].astype(F32)
-        block = jnp.floor(place * (1.0 / LANES))
-        within = place - block * LANES
-        code = jnp.where(within == iota((LANES, ROWS), 0).astype(F32), block, -1.0).T.astype(BF16)
-        hot = jnp.concatenate(
-            [jnp.where(code == jnp.bfloat16(q), 1.0, 0.0).astype(BF16) for q in range(reach * ROWS // LANES)], axis=1
-        )
-        stage_ref[:, part] = fold(mm(hot, side_ref[0 : reach * ROWS, :])).T[:steps]
+        code = code_ref[:, part]
+        hot = jnp.concatenate([jnp.where(code == jnp.bfloat16(q), 1.0, 0.0).astype(BF16) for q in range(reach)], axis=0)
+        both = mm(side_ref[:, 0 : reach * ROWS], hot)
+        stage_ref[:, part] = both[:steps] + both[steps:]
         return pltpu.make_async_copy(stage_ref.at[:, part], out_hbm.at[:, part], out_sems.at[c])
 
     def spread(reach):
@@ -377,7 +401,8 @@
         def _():
             for b in range(reach):
                 here = slice(b * ROWS, (b + 1) * ROWS)
-                side_ref[here, :] = side(r_ref[here, :])
+                turned = r_ref[here, :].T[:steps]
+                side_ref[:, here] = jnp.concatenate(halves(turned), axis=0)
             spread(reach)
 
         low = reach
@@ -420,25 +445,47 @@
     space = -(-(rows_count + 7 * arch_count + ROWS + WIN) // ROWS) * ROWS
     shape = jax.ShapeDtypeStruct
     cap = feeder_cap.reshape(1, owned)
-    duals = lax.all_gather(dual_start, "dw", axis=0, tiled=True)
-    y, pos, offs, sums, duals = pl.pallas_call(
-        first_kernel,
+    paired = block_total == 4
+    if paired:
+        far = exchange(dual_start, "dw", 2)
+    pos, label, offs = pl.pallas_call(
+        lambda *refs: rank_kernel(owned, arch_count, *refs),
+        name="rank",
+        in_specs=[hbm()] * 3,
+        out_specs=[vmem()] * 3,
+        out_shape=[
+            shape((1, rows_count), jnp.int32),
+            shape((1, rows_count), F32),
+            shape((8, LANES), jnp.int32),
+        ],
+        scratch_shapes=[
+            pltpu.SMEM((1, block_total), jnp.int32),
+            pltpu.VMEM((1, rows_count), jnp.int32),
+            pltpu.VMEM((1, rows_count), jnp.int32),
+            pltpu.SemaphoreType.DMA((3,)),
+        ],
+        compiler_params=params(),
+    )(stay(live_counts), stay(archetype.reshape(1, rows_count)), stay(feeder.reshape(1, rows_count)))
+    if paired:
+        far, offs = lax.optimization_barrier((far, offs))
+        pieces = [exchange(dual_start, "dw", 1), far, exchange(far, "dw", 1)]
+    else:
+        pieces = [lax.all_gather(dual_start, "dw", axis=0, tiled=True)]
+    y, sums, duals = pl.pallas_call(
+        lambda *refs: first_kernel(block_total, *refs),
         name="first",
-        in_specs=[hbm()] * 5 + [vmem()] * 2,
-        out_specs=[vmem()] * 5,
+        in_specs=[hbm()] * 4 + [vmem()] * (3 + len(pieces)),
+        out_specs=[vmem()] * 3,
         out_shape=[
             shape((space, LANES), F32),
-            shape((1, rows_count), jnp.int32),
-            shape((8, LANES), jnp.int32),
             shape((feeders + 8, 2 * LANES), F32),
             shape((feeders, LANES), F32),
         ],
         scratch_shapes=[
-            pltpu.VMEM((1, rows_count), jnp.int32),
-            pltpu.VMEM((1, rows_count), jnp.int32),
             pltpu.VMEM((steps, rows_count), F32),
             pltpu.VMEM((arch_count, steps, steps), F32),
-            pltpu.SMEM((1, block_total), jnp.int32),
+            pltpu.VMEM((owned, steps), F32),
+            pltpu.VMEM((1, owned), jnp.int32),
             pltpu.VMEM((rows_count, 2 * LANES), BF16),
             pltpu.VMEM((ROWS, rows_count), BF16),
             pltpu.VMEM((space, LANES), F32),
@@ -446,18 +493,10 @@
             pltpu.VMEM((space, LANES), F32),
             pltpu.VMEM((arch_count, 2 * LANES, LANES), BF16),
             pltpu.SMEM((8, LANES), jnp.int32),
-            pltpu.SemaphoreType.DMA((6,)),
+            pltpu.SemaphoreType.DMA((5,)),
         ],
         compiler_params=params(),
-    )(
-        stay(live_counts),
-        stay(archetype.reshape(1, rows_count)),
-        stay(feeder.reshape(1, rows_count)),
-        stay(load_base),
-        stay(kkt_inverse),
-        duals,
-        cap,
-    )
+    )(stay(load_base), stay(kkt_inverse), stay(dual_start), stay(cap), pos, label, offs, *pieces)
     gathered = lax.all_gather(sums, "dw", axis=0)
     pack, next_duals, rest = pl.pallas_call(
         lambda *refs: middle_kernel(steps, arch_count, *refs),
@@ -491,7 +530,9 @@
         scratch_shapes=[
             pltpu.VMEM((space, LANES), F32),
             pltpu.VMEM((space, LANES), F32),
-            pltpu.VMEM((space, 2 * LANES), BF16),
+            pltpu.VMEM((2 * steps, space), BF16),
+            pltpu.VMEM((arch_count, 2 * LANES, LANES), BF16),
+            pltpu.VMEM((ROWS, rows_count), BF16),
             pltpu.VMEM((EXTRA, LANES), F32),
             pltpu.VMEM((8, LANES), F32),
             pltpu.VMEM((steps, rows_count), F32),

time: 43.9 us -> 40.9 us (0.932); the launches traced: 43.5 us -> 41.1 us
  blocking collectives: 13 us -> 6.02 us
  starting transfers between devices: 4.63 us -> 8.06 us
  waiting for transfers between devices: 4.38 us -> 5.67 us
  local copies, waits for them, and re-layouts: 0.67 us -> 0.02 us
  Pallas kernels: 20 us -> 20.5 us
    all_gather x1 -> x0, blocking collectives: 6.52 us -> none  [on_device(): duals = lax.all_gather(dual_start, 'dw', axis=0, tiled=True)]
    ppermute x2 -> x5, starting transfers between devices: 4.63 us -> 8.06 us  [exchange(): lax.ppermute(x, axis, [(i, i ^ mask) for i in range(lax.axis_size(axis))])]
    pallas_call x1 -> x2, Pallas kernels: 10.6 us -> 12.2 us  [the longest x1 11 us: on_device(): pl.pallas_call(lambda *refs: first_kernel(block_total, *refs), name='firs...]
    ppermute x2 -> x5, waiting for transfers between devices: 4.38 us -> 5.67 us  [exchange(): lax.ppermute(x, axis, [(i, i ^ mask) for i in range(lax.axis_size(axis))])]
    pallas_call x1, Pallas kernels: 9.1 us -> 7.92 us  [on_device(): pl.pallas_call(lambda *refs: last_kernel(inv_root, *refs), name='last', i...]
    unnamed x8 -> x6, local copies, waits for them, and re-layouts: 0.67 us -> 0.02 us
  transfers between devices with their start and end apart: 2 -> 5, of which waited for: 2 -> 4; matrix products, arithmetic and copies ran while one was open for 0% -> 0% of each run, Pallas kernels for 0% -> 3%
where the time goes in v4:
time: 40.9 us; the launch traced here: 41.1 us
  Pallas kernels  20.5 us (50%)
  starting transfers between devices  8.06 us (20%)
  blocking collectives  6.02 us (15%)
  waiting for transfers between devices  5.67 us (14%)
  between operations  0.85 us (2%)
    pallas_call x1, Pallas kernels, on_device(): pl.pallas_call(lambda *refs: first_kernel(block_total, *refs), name='firs...  11 us
    ppermute x5, starting transfers between devices, exchange(): lax.ppermute(x, axis, [(i, i ^ mask) for i in range(lax.axis_size(axis))])  8.06 us
    pallas_call x1, Pallas kernels, on_device(): pl.pallas_call(lambda *refs: last_kernel(inv_root, *refs), name='last', i...  7.92 us
    all_gather x1, blocking collectives, on_device(): gathered = lax.all_gather(sums, 'dw', axis=0)  6.02 us
    ppermute x5, waiting for transfers between devices, exchange(): lax.ppermute(x, axis, [(i, i ^ mask) for i in range(lax.axis_size(axis))])  5.67 us
    pallas_call x1, Pallas kernels, on_device(): pl.pallas_call(lambda *refs: rank_kernel(owned, arch_count, *refs), name=...  1.25 us
  transfers between devices with their start and end apart: 5, of which 4 were waited for; matrix products, arithmetic and copies ran while one was open for 0% of the time, Pallas kernels for 3%

profile of v4, /device:TPU:0, one launch (start us, length us, event | category | flops | bytes accessed | tf_op | source)
XLA Modules:
  0.0 41.1 jit_solution(852651434269792878)
XLA Ops:
  0.6 0.0 copy-start
  0.6 0.0 copy-start.1
  0.7 0.0 copy-start.2
  0.7 3.0 %collective-permute-start = (f32[16,96]{1,0:T(8,128)}, f32[16,96]{1,0:T(8,128)S(1)}, u32[]{:S(2)}, u32[]{:S(2)}) collective-permute-start(f32[16,96]{1,0:T(8,128)} %refs_2_.1), channel_id=1, source_target_pairs={{0,8},{4,12},{8,0},{12,4},{1,9},{5,13},{9,1},{13,5},{2,10},{6,14},... | collective-permute-start | bytes 18440 | tf_op jit(solution)/shard_map/ppermute | solution.py:432
  3.7 0.0 collective-permute-start.1
  3.7 1.3 %rank.1 = (s32[1,2048]{1,0:T(1,128)S(1)}, f32[1,2048]{1,0:T(1,128)S(1)}, s32[8,128]{1,0:T(8,128)S(1)}) custom-call(s32[1,4]{1,0:T(1,128)} %refs_0_.2, s32[1,2048]{1,0:T(1,128)} %bitcast.10, s32[1,2048]{1,0:T(1,128)} %bitcast.11), custom_call_target="tpu_custom_call" | custom-call | tf_op jit(solution)/shard_map/rank/pallas_call | solution.py:451
  4.9 0.6 %collective-permute-done.refs_8_ = f32[16,96]{1,0:T(8,128)S(1)} collective-permute-done((f32[16,96]{1,0:T(8,128)}, f32[16,96]{1,0:T(8,128)S(1)}, u32[]{:S(2)}, u32[]{:S(2)}) %collective-permute-start) | collective-permute-done | bytes 6176 | tf_op jit(solution)/shard_map/ppermute | solution.py:432
  5.5 0.0 collective-permute-start.2
  5.5 0.0 collective-permute-done.1.refs_7_
  5.5 1.2 %collective-permute-done.2.refs_9_ = f32[16,96]{1,0:T(8,128)S(1)} collective-permute-done((f32[16,96]{1,0:T(8,128)S(1)}, f32[16,96]{1,0:T(8,128)S(1)}, u32[]{:S(2)}, u32[]{:S(2)}) %collective-permute-start.2) | collective-permute-done | bytes 6176 | tf_op jit(solution)/shard_map/ppermute | solution.py:432
  6.7 11.0 %first.1 = (f32[2816,128]{1,0:T(8,128)S(1)}, f32[72,256]{1,0:T(8,128)S(1)}, f32[64,128]{1,0:T(8,128)S(1)}) custom-call(f32[96,2048]{1,0:T(8,128)} %refs_0_.3, f32[64,96,96]{2,1,0:T(8,128)} %refs_8_.1, f32[16,96]{1,0:T(8,128)} %refs_2_.1, s32[1,16]{1,0:T(1,128)} %bitcast.7, s32[1,2048]{1,0:T(1,128)S(1)} %get-tuple-element.19.refs_4_.refs_3_, ...), custom_call_target="tpu_custom_call" | custom-call | tf_op jit(solution)/shard_map/first/pallas_call | solution.py:474
  17.7 6.0 %all-gather = f32[288,256]{1,0:T(8,128)S(1)} all-gather(f32[72,256]{1,0:T(8,128)S(1)} %get-tuple-element.23), channel_id=2, replica_groups=mesh['scen'=2,'dw'=4,'reg'=4] {'dw'}, dimensions={0}, use_global_device_ids=true | all-gather | bytes 368640 | tf_op jit(solution)/shard_map/all_gather | solution.py:500
  23.7 0.3 middle.1
  24.0 2.0 %collective-permute-start.3 = (f32[72,128]{1,0:T(8,128)S(1)}, f32[72,128]{1,0:T(8,128)S(1)}, u32[]{:S(2)}, u32[]{:S(2)}) collective-permute-start(f32[72,128]{1,0:T(8,128)S(1)} %get-tuple-element.27), channel_id=1, source_target_pairs={{0,1},{1,0},{2,3},{3,2},{4,5},{5,4},{6,7},{7,6},{8,9},{9,8},{10,11... | collective-permute-start | bytes 110600 | tf_op jit(solution)/shard_map/ppermute | solution.py:432
  26.1 2.0 %collective-permute-done.3 = f32[72,128]{1,0:T(8,128)S(1)} collective-permute-done((f32[72,128]{1,0:T(8,128)S(1)}, f32[72,128]{1,0:T(8,128)S(1)}, u32[]{:S(2)}, u32[]{:S(2)}) %collective-permute-start.3) | collective-permute-done | bytes 36896 | tf_op jit(solution)/shard_map/ppermute | solution.py:432
  28.1 3.0 %collective-permute-start.4 = (f32[72,128]{1,0:T(8,128)S(1)}, f32[72,128]{1,0:T(8,128)S(1)}, u32[]{:S(2)}, u32[]{:S(2)}) collective-permute-start(f32[72,128]{1,0:T(8,128)S(1)} %add.3.refs_6_), channel_id=1, source_target_pairs={{0,2},{1,3},{2,0},{3,1},{4,6},{5,7},{6,4},{7,5},{8,10},{9,11},{10,... | collective-permute-start | bytes 110600 | tf_op jit(solution)/shard_map/ppermute | solution.py:432
  31.1 1.9 %collective-permute-done.4.refs_7_ = f32[72,128]{1,0:T(8,128)S(1)} collective-permute-done((f32[72,128]{1,0:T(8,128)S(1)}, f32[72,128]{1,0:T(8,128)S(1)}, u32[]{:S(2)}, u32[]{:S(2)}) %collective-permute-start.4) | collective-permute-done | bytes 36896 | tf_op jit(solution)/shard_map/ppermute | solution.py:432
  33.0 0.0 copy-done
  33.0 0.0 copy-done.1
  33.0 0.0 copy-done.2
  33.0 7.9 %last.1 = (f32[96,2048]{1,0:T(8,128)}, f32[16,96]{1,0:T(8,128)}, f32[1,96]{1,0:T(1,128)}) custom-call(s32[1,16]{1,0:T(1,128)S(1)} %bitcast.8, s32[8,128]{1,0:T(8,128)S(1)} %get-tuple-element.18.refs_6_.refs_1_, f32[2816,128]{1,0:T(8,128)S(1)} %get-tuple-element.22.refs_2_, s32[1,2048]{1,0:T(1,128)S(1)} %get-tuple-element.19.refs_4_.refs_3_, ...), custom_call_target="tpu_custom_call" | custom-call | tf_op jit(solution)/shard_map/last/pallas_call | solution.py:520
  (1 shorter events, 0.0 us)
Async XLA Ops:
  0.6 32.4 %copy-start = (f32[64,96,96]{2,1,0:T(8,128)S(1)}, f32[64,96,96]{2,1,0:T(8,128)}, u32[]{:S(2)}) copy-start(f32[64,96,96]{2,1,0:T(8,128)} %refs_8_.1) | copy-start | bytes 7077892
  0.6 32.4 %copy-start.1 = (s32[16]{0:T(128)S(1)}, s32[16]{0:T(128)}, u32[]{:S(2)}) copy-start(s32[16]{0:T(128)} %param.13) | copy-start | bytes 196
  0.7 32.4 %copy-start.2 = (f32[96]{0:T(128)S(1)}, f32[96]{0:T(128)}, u32[]{:S(2)}) copy-start(f32[96]{0:T(128)} %param.15) | copy-start | bytes 1156
  0.7 4.8 %collective-permute-start = (f32[16,96]{1,0:T(8,128)}, f32[16,96]{1,0:T(8,128)S(1)}, u32[]{:S(2)}, u32[]{:S(2)}) collective-permute-start(f32[16,96]{1,0:T(8,128)} %refs_2_.1), channel_id=1, source_target_pairs={{0,8},{4,12},{8,0},{12,4},{1,9},{5,13},{9,1},{13,5},{2,10},{6,14},... | collective-permute-start | bytes 18440 | tf_op jit(solution)/shard_map/ppermute | solution.py:432
  3.7 1.8 %collective-permute-start.1 = (f32[16,96]{1,0:T(8,128)}, f32[16,96]{1,0:T(8,128)S(1)}, u32[]{:S(2)}, u32[]{:S(2)}) collective-permute-start(f32[16,96]{1,0:T(8,128)} %refs_2_.1), channel_id=1, source_target_pairs={{0,4},{4,0},{8,12},{12,8},{1,5},{5,1},{9,13},{13,9},{2,6},{6,2},{1... | collective-permute-start | bytes 18440 | tf_op jit(solution)/shard_map/ppermute | solution.py:432
  5.5 1.2 %collective-permute-start.2 = (f32[16,96]{1,0:T(8,128)S(1)}, f32[16,96]{1,0:T(8,128)S(1)}, u32[]{:S(2)}, u32[]{:S(2)}) collective-permute-start(f32[16,96]{1,0:T(8,128)S(1)} %collective-permute-done.refs_8_), channel_id=1, source_target_pairs={{0,4},{4,0},{8,12},{12,8},{1,5},{5,1},{9,13},{13,9},{2,6},{6,2},{1... | collective-permute-start | bytes 18440 | tf_op jit(solution)/shard_map/ppermute | solution.py:432
  24.0 4.0 %collective-permute-start.3 = (f32[72,128]{1,0:T(8,128)S(1)}, f32[72,128]{1,0:T(8,128)S(1)}, u32[]{:S(2)}, u32[]{:S(2)}) collective-permute-start(f32[72,128]{1,0:T(8,128)S(1)} %get-tuple-element.27), channel_id=1, source_target_pairs={{0,1},{1,0},{2,3},{3,2},{4,5},{5,4},{6,7},{7,6},{8,9},{9,8},{10,11... | collective-permute-start | bytes 110600 | tf_op jit(solution)/shard_map/ppermute | solution.py:432
  28.1 4.9 %collective-permute-start.4 = (f32[72,128]{1,0:T(8,128)S(1)}, f32[72,128]{1,0:T(8,128)S(1)}, u32[]{:S(2)}, u32[]{:S(2)}) collective-permute-start(f32[72,128]{1,0:T(8,128)S(1)} %add.3.refs_6_), channel_id=1, source_target_pairs={{0,2},{1,3},{2,0},{3,1},{4,6},{5,7},{6,4},{7,5},{8,10},{9,11},{10,... | collective-permute-start | bytes 110600 | tf_op jit(solution)/shard_map/ppermute | solution.py:432

commit v5 on v4

--- a/solution.py
+++ b/solution.py
@@ -15,7 +15,7 @@
 ROWS = 256
 WIN = 48
 BLOCKS = 8
-EXTRA = 32
+EXTRA = 24
 VMEM_BYTES = 24 * 1024 * 1024
 
 F32 = jnp.float32
@@ -56,9 +56,9 @@
 def split_matrices(kkt_ref, mat_ref):
     arch_count, steps, _ = kkt_ref.shape
     for a in range(arch_count):
-        high, low = halves(kkt_ref[a])
+        high, low = halves(kkt_ref[a].T)
         mat_ref[a, 0:steps, 0:steps] = high
-        mat_ref[a, LANES : LANES + steps, 0:steps] = low
+        mat_ref[a, 0:steps, LANES : LANES + steps] = low
 
 
 def row_code(place):
@@ -69,9 +69,8 @@
 
 def apply_matrix(x, matrix):
     count = x.shape[0]
-    x = x[:, : matrix.shape[1]]
     rest = x - x.astype(BF16).astype(F32)
-    both = mm(jnp.concatenate([x, rest], axis=0).astype(BF16), matrix, NT)
+    both = mm(jnp.concatenate([x, rest], axis=0).astype(BF16), matrix)
     return both[:count, :LANES] + (both[count:, :LANES] + both[:count, LANES:])
 
 
@@ -228,13 +227,13 @@
     copies[1].wait()
     split_matrices(kkt_ref, mat_ref)
 
-    def permute(b, inner):
-        at = pl.multiple_of(b * ROWS, ROWS)
-        hot = jnp.where(code_ref[...] == b.astype(F32).astype(BF16), 1.0, 0.0).astype(BF16)
+    def permute(at, inner):
+        number = jnp.asarray(at // ROWS, jnp.int32).astype(F32).astype(BF16)
+        hot = jnp.where(code_ref[...] == number, 1.0, 0.0).astype(BF16)
         xs_ref[pl.ds(at, ROWS), :] = fold(mm(hot, xt_ref[...]))
         return inner
 
-    lax.fori_loop(0, blocks, permute, 0)
+    each_block(blocks, permute, 0)
 
     def pick(at, inner):
         here = pl.ds(at, ROWS)
@@ -388,11 +387,11 @@
 
     def spread(reach):
         def pair(c, inner):
-            for half in range(2):
-                columns(2 * c + half, reach).start()
+            for part in range(4):
+                columns(4 * c + part, reach).start()
             return inner
 
-        lax.fori_loop(0, rows_count // (2 * ROWS), pair, 0)
+        lax.fori_loop(0, rows_count // (4 * ROWS), pair, 0)
 
     count = blocks
     low = 0
@@ -491,7 +490,7 @@
             pltpu.VMEM((space, LANES), F32),
             pltpu.VMEM((space, LANES), F32),
             pltpu.VMEM((space, LANES), F32),
-            pltpu.VMEM((arch_count, 2 * LANES, LANES), BF16),
+            pltpu.VMEM((arch_count, LANES, 2 * LANES), BF16),
             pltpu.SMEM((8, LANES), jnp.int32),
             pltpu.SemaphoreType.DMA((5,)),
         ],
@@ -531,7 +530,7 @@
             pltpu.VMEM((space, LANES), F32),
             pltpu.VMEM((space, LANES), F32),
             pltpu.VMEM((2 * steps, space), BF16),
-            pltpu.VMEM((arch_count, 2 * LANES, LANES), BF16),
+            pltpu.VMEM((arch_count, LANES, 2 * LANES), BF16),
             pltpu.VMEM((ROWS, rows_count), BF16),
             pltpu.VMEM((EXTRA, LANES), F32),
             pltpu.VMEM((8, LANES), F32),

time: 40.9 us -> 38.8 us (0.949)
  Pallas kernels: 20.5 us -> 17.9 us
  starting transfers between devices: 8.06 us -> 7.22 us
  waiting for transfers between devices: 5.67 us -> 6.42 us
  blocking collectives: 6.02 us -> 6.47 us
    pallas_call x1, Pallas kernels: 11 us -> 8.8 us  [on_device(): pl.pallas_call(lambda *refs: first_kernel(block_total, *refs), name='firs...]
    ppermute x5, starting transfers between devices: 8.06 us -> 7.22 us  [exchange(): lax.ppermute(x, axis, [(i, i ^ mask) for i in range(lax.axis_size(axis))])]
    ppermute x5, waiting for transfers between devices: 5.67 us -> 6.42 us  [exchange(): lax.ppermute(x, axis, [(i, i ^ mask) for i in range(lax.axis_size(axis))])]
    all_gather x1, blocking collectives: 6.02 us -> 6.47 us  [on_device(): gathered = lax.all_gather(sums, 'dw', axis=0)]
    pallas_call x1, Pallas kernels: 7.92 us -> 7.49 us  [on_device(): pl.pallas_call(lambda *refs: last_kernel(inv_root, *refs), name='last', i...]
where the time goes in v5:
time: 38.8 us
  Pallas kernels  17.9 us (46%)
  starting transfers between devices  7.22 us (19%)
  blocking collectives  6.47 us (17%)
  waiting for transfers between devices  6.42 us (17%)
  between operations  0.85 us (2%)
    pallas_call x1, Pallas kernels, on_device(): pl.pallas_call(lambda *refs: first_kernel(block_total, *refs), name='firs...  8.8 us
    pallas_call x1, Pallas kernels, on_device(): pl.pallas_call(lambda *refs: last_kernel(inv_root, *refs), name='last', i...  7.49 us
    ppermute x5, starting transfers between devices, exchange(): lax.ppermute(x, axis, [(i, i ^ mask) for i in range(lax.axis_size(axis))])  7.22 us
    all_gather x1, blocking collectives, on_device(): gathered = lax.all_gather(sums, 'dw', axis=0)  6.47 us
    ppermute x5, waiting for transfers between devices, exchange(): lax.ppermute(x, axis, [(i, i ^ mask) for i in range(lax.axis_size(axis))])  6.42 us
    pallas_call x1, Pallas kernels, on_device(): pl.pallas_call(lambda *refs: rank_kernel(owned, arch_count, *refs), name=...  1.25 us
  transfers between devices with their start and end apart: 5, of which 4 were waited for; matrix products, arithmetic and copies ran while one was open for 0% of the time, Pallas kernels for 3%

profile of v5, /device:TPU:0, one launch (start us, length us, event | category | flops | bytes accessed | tf_op | source)
XLA Modules:
  0.0 38.8 jit_solution(17900002812092424648)
XLA Ops:
  0.6 0.0 copy-start
  0.6 0.0 copy-start.1
  0.7 0.0 copy-start.2
  0.7 3.0 %collective-permute-start = (f32[16,96]{1,0:T(8,128)}, f32[16,96]{1,0:T(8,128)S(1)}, u32[]{:S(2)}, u32[]{:S(2)}) collective-permute-start(f32[16,96]{1,0:T(8,128)} %refs_2_.1), channel_id=1, source_target_pairs={{0,8},{4,12},{8,0},{12,4},{1,9},{5,13},{9,1},{13,5},{2,10},{6,14},... | collective-permute-start | bytes 18440 | tf_op jit(solution)/shard_map/ppermute | solution.py:431
  3.7 0.0 collective-permute-start.1
  3.7 1.3 %rank.1 = (s32[1,2048]{1,0:T(1,128)S(1)}, f32[1,2048]{1,0:T(1,128)S(1)}, s32[8,128]{1,0:T(8,128)S(1)}) custom-call(s32[1,4]{1,0:T(1,128)} %refs_0_.2, s32[1,2048]{1,0:T(1,128)} %bitcast.10, s32[1,2048]{1,0:T(1,128)} %bitcast.11), custom_call_target="tpu_custom_call" | custom-call | tf_op jit(solution)/shard_map/rank/pallas_call | solution.py:450
  4.9 0.6 %collective-permute-done.refs_8_ = f32[16,96]{1,0:T(8,128)S(1)} collective-permute-done((f32[16,96]{1,0:T(8,128)}, f32[16,96]{1,0:T(8,128)S(1)}, u32[]{:S(2)}, u32[]{:S(2)}) %collective-permute-start) | collective-permute-done | bytes 6176 | tf_op jit(solution)/shard_map/ppermute | solution.py:431
  5.5 0.0 collective-permute-start.2
  5.5 0.0 collective-permute-done.1.refs_7_
  5.5 1.2 %collective-permute-done.2.refs_9_ = f32[16,96]{1,0:T(8,128)S(1)} collective-permute-done((f32[16,96]{1,0:T(8,128)S(1)}, f32[16,96]{1,0:T(8,128)S(1)}, u32[]{:S(2)}, u32[]{:S(2)}) %collective-permute-start.2) | collective-permute-done | bytes 6176 | tf_op jit(solution)/shard_map/ppermute | solution.py:431
  6.7 8.8 %first.1 = (f32[2816,128]{1,0:T(8,128)S(1)}, f32[72,256]{1,0:T(8,128)S(1)}, f32[64,128]{1,0:T(8,128)S(1)}) custom-call(f32[96,2048]{1,0:T(8,128)} %refs_0_.3, f32[64,96,96]{2,1,0:T(8,128)} %refs_8_.1, f32[16,96]{1,0:T(8,128)} %refs_2_.1, s32[1,16]{1,0:T(1,128)} %bitcast.7, s32[1,2048]{1,0:T(1,128)S(1)} %get-tuple-element.19.refs_4_.refs_3_, ...), custom_call_target="tpu_custom_call" | custom-call | tf_op jit(solution)/shard_map/first/pallas_call | solution.py:473
  15.5 6.5 %all-gather = f32[288,256]{1,0:T(8,128)S(1)} all-gather(f32[72,256]{1,0:T(8,128)S(1)} %get-tuple-element.23), channel_id=2, replica_groups=mesh['scen'=2,'dw'=4,'reg'=4] {'dw'}, dimensions={0}, use_global_device_ids=true | all-gather | bytes 368640 | tf_op jit(solution)/shard_map/all_gather | solution.py:499
  22.0 0.3 middle.1
  22.3 1.6 %collective-permute-start.3 = (f32[72,128]{1,0:T(8,128)S(1)}, f32[72,128]{1,0:T(8,128)S(1)}, u32[]{:S(2)}, u32[]{:S(2)}) collective-permute-start(f32[72,128]{1,0:T(8,128)S(1)} %get-tuple-element.27), channel_id=1, source_target_pairs={{0,1},{1,0},{2,3},{3,2},{4,5},{5,4},{6,7},{7,6},{8,9},{9,8},{10,11... | collective-permute-start | bytes 110600 | tf_op jit(solution)/shard_map/ppermute | solution.py:431
  23.9 2.4 %collective-permute-done.3 = f32[72,128]{1,0:T(8,128)S(1)} collective-permute-done((f32[72,128]{1,0:T(8,128)S(1)}, f32[72,128]{1,0:T(8,128)S(1)}, u32[]{:S(2)}, u32[]{:S(2)}) %collective-permute-start.3) | collective-permute-done | bytes 36896 | tf_op jit(solution)/shard_map/ppermute | solution.py:431
  26.3 2.6 %collective-permute-start.4 = (f32[72,128]{1,0:T(8,128)S(1)}, f32[72,128]{1,0:T(8,128)S(1)}, u32[]{:S(2)}, u32[]{:S(2)}) collective-permute-start(f32[72,128]{1,0:T(8,128)S(1)} %add.3.refs_6_), channel_id=1, source_target_pairs={{0,2},{1,3},{2,0},{3,1},{4,6},{5,7},{6,4},{7,5},{8,10},{9,11},{10,... | collective-permute-start | bytes 110600 | tf_op jit(solution)/shard_map/ppermute | solution.py:431
  28.9 2.3 %collective-permute-done.4.refs_7_ = f32[72,128]{1,0:T(8,128)S(1)} collective-permute-done((f32[72,128]{1,0:T(8,128)S(1)}, f32[72,128]{1,0:T(8,128)S(1)}, u32[]{:S(2)}, u32[]{:S(2)}) %collective-permute-start.4) | collective-permute-done | bytes 36896 | tf_op jit(solution)/shard_map/ppermute | solution.py:431
  31.2 0.0 copy-done
  31.2 0.0 copy-done.1
  31.2 0.0 copy-done.2
  31.2 7.5 %last.1 = (f32[96,2048]{1,0:T(8,128)}, f32[16,96]{1,0:T(8,128)}, f32[1,96]{1,0:T(1,128)}) custom-call(s32[1,16]{1,0:T(1,128)S(1)} %bitcast.8, s32[8,128]{1,0:T(8,128)S(1)} %get-tuple-element.18.refs_6_.refs_1_, f32[2816,128]{1,0:T(8,128)S(1)} %get-tuple-element.22.refs_2_, s32[1,2048]{1,0:T(1,128)S(1)} %get-tuple-element.19.refs_4_.refs_3_, ...), custom_call_target="tpu_custom_call" | custom-call | tf_op jit(solution)/shard_map/last/pallas_call | solution.py:519
  (1 shorter events, 0.0 us)
Async XLA Ops:
  0.6 30.6 %copy-start = (f32[64,96,96]{2,1,0:T(8,128)S(1)}, f32[64,96,96]{2,1,0:T(8,128)}, u32[]{:S(2)}) copy-start(f32[64,96,96]{2,1,0:T(8,128)} %refs_8_.1) | copy-start | bytes 7077892
  0.6 30.5 %copy-start.1 = (s32[16]{0:T(128)S(1)}, s32[16]{0:T(128)}, u32[]{:S(2)}) copy-start(s32[16]{0:T(128)} %param.13) | copy-start | bytes 196
  0.7 30.5 %copy-start.2 = (f32[96]{0:T(128)S(1)}, f32[96]{0:T(128)}, u32[]{:S(2)}) copy-start(f32[96]{0:T(128)} %param.15) | copy-start | bytes 1156
  0.7 4.8 %collective-permute-start = (f32[16,96]{1,0:T(8,128)}, f32[16,96]{1,0:T(8,128)S(1)}, u32[]{:S(2)}, u32[]{:S(2)}) collective-permute-start(f32[16,96]{1,0:T(8,128)} %refs_2_.1), channel_id=1, source_target_pairs={{0,8},{4,12},{8,0},{12,4},{1,9},{5,13},{9,1},{13,5},{2,10},{6,14},... | collective-permute-start | bytes 18440 | tf_op jit(solution)/shard_map/ppermute | solution.py:431
  3.7 1.8 %collective-permute-start.1 = (f32[16,96]{1,0:T(8,128)}, f32[16,96]{1,0:T(8,128)S(1)}, u32[]{:S(2)}, u32[]{:S(2)}) collective-permute-start(f32[16,96]{1,0:T(8,128)} %refs_2_.1), channel_id=1, source_target_pairs={{0,4},{4,0},{8,12},{12,8},{1,5},{5,1},{9,13},{13,9},{2,6},{6,2},{1... | collective-permute-start | bytes 18440 | tf_op jit(solution)/shard_map/ppermute | solution.py:431
  5.5 1.2 %collective-permute-start.2 = (f32[16,96]{1,0:T(8,128)S(1)}, f32[16,96]{1,0:T(8,128)S(1)}, u32[]{:S(2)}, u32[]{:S(2)}) collective-permute-start(f32[16,96]{1,0:T(8,128)S(1)} %collective-permute-done.refs_8_), channel_id=1, source_target_pairs={{0,4},{4,0},{8,12},{12,8},{1,5},{5,1},{9,13},{13,9},{2,6},{6,2},{1... | collective-permute-start | bytes 18440 | tf_op jit(solution)/shard_map/ppermute | solution.py:431
  22.3 4.0 %collective-permute-start.3 = (f32[72,128]{1,0:T(8,128)S(1)}, f32[72,128]{1,0:T(8,128)S(1)}, u32[]{:S(2)}, u32[]{:S(2)}) collective-permute-start(f32[72,128]{1,0:T(8,128)S(1)} %get-tuple-element.27), channel_id=1, source_target_pairs={{0,1},{1,0},{2,3},{3,2},{4,5},{5,4},{6,7},{7,6},{8,9},{9,8},{10,11... | collective-permute-start | bytes 110600 | tf_op jit(solution)/shard_map/ppermute | solution.py:431
  26.3 4.9 %collective-permute-start.4 = (f32[72,128]{1,0:T(8,128)S(1)}, f32[72,128]{1,0:T(8,128)S(1)}, u32[]{:S(2)}, u32[]{:S(2)}) collective-permute-start(f32[72,128]{1,0:T(8,128)S(1)} %add.3.refs_6_), channel_id=1, source_target_pairs={{0,2},{1,3},{2,0},{3,1},{4,6},{5,7},{6,4},{7,5},{8,10},{9,11},{10,... | collective-permute-start | bytes 110600 | tf_op jit(solution)/shard_map/ppermute | solution.py:431
